TPU v7x, 256 devices: a whole 4x4x8 slice. The times are simulated.
256 devices in a mesh: row: 32 (over x, y, core), col: 8 (over z).
Axes of the slice: x: 4, y: 4, z: 8, core: 2. Of those that a mesh axis runs over, the one named last changes fastest.
Arguments:
- kernel_tiles: float32 [32, 8, 9, 256, 512], P('row', 'col'), may hold values from -0.09375 to 0.09375
- footprints: int32 [32, 8, 9], P('row', 'col'), may hold values from 0 to 8, as said below
- counts: int32 [32, 8], P('row', 'col'), may hold values from 64 to 256, as said below
- readings: float32 [32, 8, 256], P('row', 'col'), may hold values from -6 to 6
- damping: float32 [1], replicated, may hold values from 0.1 to 0.5
- layer_depth: float32 [2], replicated, may hold values from 1 to 6
- inclinations: float32 [2], replicated, may hold values from 0.6 to 1.3
- declinations: float32 [2], replicated, may hold values from -3.140625 to 3.140625
- resid_grid: float32 [4096, 4096], P('col', 'row'), may hold values from -3 to 3
Outputs:
- coefficients: float32 [32, 8, 512], P('row', 'col')
- rtp_map: float32 [4096, 4096], P(('row', 'col'))
Inputs may be any that keep to these rules, and one draw needn't show every extreme that they name: `footprints`: each tile's list holds each of the 9 codes once; code 3 (a + 1) + (b + 1) names the source block a tiles north and b tiles east of the tile; blocks outside the survey are empty. `counts`: reading slots from this count on are ignored.
All inputs are finite; a program needn't handle non-finite values.
Results may differ from a plain program's by a relative error of at most 0.0003.
Values sent between devices are 32-bit elements; how exact they have to be, the bound alone decides.
A program may use at most 128 MiB of HBM per device.

v0:
```python
import math

import jax
import jax.numpy as jnp
from jax import lax
from jax.sharding import PartitionSpec as P

SRC_ROWS = 8
SRC_COLS = 32
LAYERS = 2
REFINE = 16
INNER_LEN = 128
FOOTPRINT = 9
CG_STEPS = 2


HIGHEST_PRECISION = lax.Precision.HIGHEST
NEIGHBOUR_OFFSETS = tuple(
    ((north_step, east_step) for north_step in (-1, 0, 1) for east_step in (-1, 0, 1))
)


def shifted(x, axis, by):
    peers = lax.axis_size(axis)
    pairs = [(i, i + by) for i in range(peers) if 0 <= i + by < peers]
    return lax.ppermute(x, axis, pairs)


def hat_table(fine_start, fine_count, coarse_start, coarse_count):
    fine_pos = jnp.arange(fine_count, dtype=jnp.float32) + fine_start
    coarse_pos = jnp.arange(coarse_count, dtype=jnp.float32) + coarse_start
    offset = (fine_pos[:, None] + 0.5) / REFINE - 0.5 - coarse_pos[None, :]
    return jnp.maximum(0.0, 1.0 - jnp.abs(offset))


def frequency_of(positions, full_len):
    signed = jnp.where(positions < full_len // 2, positions, positions - full_len)
    return signed.astype(jnp.float32) / full_len


def pole_filter(north_freq, east_freq, inclinations, declinations):
    radius = jnp.sqrt(north_freq * north_freq + east_freq * east_freq)
    safe_radius = jnp.where(radius > 0.0, radius, 1.0)
    unit_north = jnp.where(radius > 0.0, north_freq / safe_radius, 0.0)
    unit_east = jnp.where(radius > 0.0, east_freq / safe_radius, 0.0)
    real_part = jnp.ones_like(radius)
    imag_part = jnp.zeros_like(radius)
    for member in range(2):
        vertical = jnp.sin(inclinations[member])
        horizontal = jnp.cos(inclinations[member])
        along_axis = horizontal * (
            jnp.cos(declinations[member]) * unit_north + jnp.sin(declinations[member]) * unit_east
        )
        denominator = vertical * vertical + along_axis * along_axis
        inv_real = vertical / denominator
        inv_imag = -along_axis / denominator
        real_part, imag_part = (
            real_part * inv_real - imag_part * inv_imag,
            real_part * inv_imag + imag_part * inv_real,
        )
    return (real_part, imag_part)


def phase_table(row_len, col_len, period, direction_sign):
    product = (
        jnp.arange(row_len, dtype=jnp.int32)[:, None]
        * jnp.arange(col_len, dtype=jnp.int32)[None, :]
        % period
    )
    angle = 2.0 * math.pi / period * product.astype(jnp.float32)
    return (jnp.cos(angle), direction_sign * jnp.sin(angle))


def transform_last(real_in, imag_in, direction_sign):
    dims_in = real_in.shape
    length = dims_in[-1]
    outer_len = length // INNER_LEN
    real_blocks = real_in.reshape(-1, outer_len, INNER_LEN)
    cos_outer, sin_outer = phase_table(outer_len, outer_len, outer_len, direction_sign)
    first_real = jnp.einsum("man,ak->mkn", real_blocks, cos_outer, precision=HIGHEST_PRECISION)
    first_imag = jnp.einsum("man,ak->mkn", real_blocks, sin_outer, precision=HIGHEST_PRECISION)
    if imag_in is not None:
        imag_blocks = imag_in.reshape(-1, outer_len, INNER_LEN)
        first_real = first_real - jnp.einsum(
            "man,ak->mkn", imag_blocks, sin_outer, precision=HIGHEST_PRECISION
        )
        first_imag = first_imag + jnp.einsum(
            "man,ak->mkn", imag_blocks, cos_outer, precision=HIGHEST_PRECISION
        )
    twist_cos, twist_sin = phase_table(outer_len, INNER_LEN, length, direction_sign)
    turned_real = first_real * twist_cos - first_imag * twist_sin
    turned_imag = first_real * twist_sin + first_imag * twist_cos
    cos_inner, sin_inner = phase_table(INNER_LEN, INNER_LEN, INNER_LEN, direction_sign)
    final_real = jnp.einsum(
        "mkn,nj->mjk", turned_real, cos_inner, precision=HIGHEST_PRECISION
    ) - jnp.einsum("mkn,nj->mjk", turned_imag, sin_inner, precision=HIGHEST_PRECISION)
    final_imag = jnp.einsum(
        "mkn,nj->mjk", turned_real, sin_inner, precision=HIGHEST_PRECISION
    ) + jnp.einsum("mkn,nj->mjk", turned_imag, cos_inner, precision=HIGHEST_PRECISION)
    return (final_real.reshape(dims_in), final_imag.reshape(dims_in))


def neighbour_block(values, step_by, keep_mask):
    arrived = shifted(values, ("row", "col"), step_by)
    return jnp.where(keep_mask, arrived, 0.0)


def collect_blocks(own_block, col_count, col_index):
    pieces = []
    for north_step, east_step in NEIGHBOUR_OFFSETS:
        if north_step == 0 and east_step == 0:
            pieces.append(own_block)
        else:
            source_col = col_index + east_step
            keep_mask = (source_col >= 0) & (source_col < col_count)
            pieces.append(
                neighbour_block(own_block, -(north_step * col_count + east_step), keep_mask)
            )
    return jnp.stack(pieces)


def return_blocks(spread, col_count, col_index):
    summed = spread[4]
    for position, (north_step, east_step) in enumerate(NEIGHBOUR_OFFSETS):
        if north_step != 0 or east_step != 0:
            source_col = col_index - east_step
            keep_mask = (source_col >= 0) & (source_col < col_count)
            summed = summed + neighbour_block(
                spread[position], north_step * col_count + east_step, keep_mask
            )
    return summed


def local_coarse(solution, col_count, col_index):
    final_blocks = collect_blocks(solution, col_count, col_index)
    coarse = final_blocks.reshape(3, 3, LAYERS, SRC_ROWS, SRC_COLS).transpose(2, 0, 3, 1, 4)
    return coarse.reshape(LAYERS, 3 * SRC_ROWS, 3 * SRC_COLS)


def squares(residual):
    return lax.psum(jnp.sum(residual * residual), ("row", "col"))


def on_device(
    kernel_tiles,
    footprints,
    counts,
    readings,
    damping,
    layer_depth,
    inclinations,
    declinations,
    resid_grid,
):
    col_count = lax.axis_size("col")
    row_count = lax.axis_size("row")
    col_index = lax.axis_index("col")
    row_index = lax.axis_index("row")
    kernels = kernel_tiles[0, 0]
    selector = (
        footprints[0, 0][:, None] == jnp.arange(FOOTPRINT, dtype=jnp.int32)[None, :]
    ).astype(jnp.float32)
    live_mask = (jnp.arange(kernels.shape[1], dtype=jnp.int32) < counts[0, 0]).astype(jnp.float32)
    ridge_weight = damping[0]

    def adjoint(values):
        partial_sums = jnp.einsum(
            "krs,r->ks", kernels, live_mask * values, precision=HIGHEST_PRECISION
        )
        spread = jnp.dot(selector.T, partial_sums, precision=HIGHEST_PRECISION)
        return return_blocks(spread, col_count, col_index)

    right_side = adjoint(readings[0, 0])
    solution = jnp.zeros_like(right_side)
    residual = right_side
    direction = right_side
    norm_now = squares(residual)
    for iteration in range(CG_STEPS):
        blocks = collect_blocks(direction, col_count, col_index)
        chosen = jnp.dot(selector, blocks, precision=HIGHEST_PRECISION)
        applied = (
            adjoint(
                live_mask * jnp.einsum("krs,ks->r", kernels, chosen, precision=HIGHEST_PRECISION)
            )
            + ridge_weight * direction
        )
        step_size = norm_now / lax.psum(jnp.sum(direction * applied), ("row", "col"))
        solution = solution + step_size * direction
        residual = residual - step_size * applied
        if iteration + 1 < CG_STEPS:
            norm_next = squares(residual)
            direction = residual + norm_next / norm_now * direction
            norm_now = norm_next
    tile_east, tile_north = resid_grid.shape
    slab_rows = tile_north // col_count
    coarse = local_coarse(solution, col_count, col_index)
    up_north = hat_table(0.0, tile_north, -float(SRC_ROWS), 3 * SRC_ROWS)
    up_east = hat_table(0.0, tile_east, -float(SRC_COLS), 3 * SRC_COLS)
    eastward = jnp.einsum("lgh,vh->lgv", coarse, up_east, precision=HIGHEST_PRECISION)
    model_planes = jnp.einsum("lgv,ug->lvu", eastward, up_north, precision=HIGHEST_PRECISION)
    tile_planes = jnp.concatenate([model_planes, resid_grid[None]], axis=0)
    planes = lax.all_to_all(tile_planes, "row", split_axis=1, concat_axis=2, tiled=True)
    full_north = planes.shape[-1]
    north_real, north_imag = transform_last(planes, None, -1.0)
    spectra = jnp.stack([north_real, north_imag])
    slab = lax.all_to_all(
        lax.all_to_all(spectra, "row", split_axis=3, concat_axis=2, tiled=True),
        "col",
        split_axis=3,
        concat_axis=2,
        tiled=True,
    )
    slab = jnp.swapaxes(slab, 2, 3)
    full_east = slab.shape[3]
    east_real, east_imag = transform_last(slab[0], slab[1], -1.0)
    north_index = (
        row_index * tile_north + col_index * slab_rows + jnp.arange(slab_rows, dtype=jnp.int32)
    )
    north_freq = frequency_of(north_index, full_north)[:, None]
    east_freq = frequency_of(jnp.arange(full_east, dtype=jnp.int32), full_east)[None, :]
    wavenumber = 2.0 * math.pi * jnp.sqrt(north_freq * north_freq + east_freq * east_freq)
    combined_real = east_real[-1]
    combined_imag = east_imag[-1]
    for layer in range(LAYERS):
        layer_real, layer_imag = (east_real[layer], east_imag[layer])
        damped = jnp.exp(-wavenumber * layer_depth[layer])
        combined_real = combined_real + damped * layer_real
        combined_imag = combined_imag + damped * layer_imag
    filt_real, filt_imag = pole_filter(north_freq, east_freq, inclinations, declinations)
    shaped_real = filt_real * combined_real - filt_imag * combined_imag
    shaped_imag = filt_real * combined_imag + filt_imag * combined_real
    back_real, back_imag = transform_last(shaped_real, shaped_imag, 1.0)
    stacked = jnp.stack([back_real, back_imag]) / full_east
    returned = lax.all_to_all(
        lax.all_to_all(stacked, "row", split_axis=2, concat_axis=1, tiled=True),
        "col",
        split_axis=2,
        concat_axis=1,
        tiled=True,
    )
    returned = jnp.swapaxes(returned, 1, 2)
    out_cols = returned.shape[1]
    ordered = returned.reshape(2, out_cols, col_count, row_count, slab_rows).transpose(
        0, 1, 3, 2, 4
    )
    ordered = ordered.reshape(2, out_cols, full_north)
    final_real, final_imag = transform_last(ordered[0], ordered[1], 1.0)
    rtp_map = final_real / full_north
    return (solution.reshape(1, 1, -1), rtp_map)


def solution(mesh):
    in_specs = (
        P("row", "col", None, None, None),
        P("row", "col", None),
        P("row", "col"),
        P("row", "col", None),
        P(),
        P(),
        P(),
        P(),
        P("col", "row"),
    )
    out_specs = (P("row", "col", None), P(("row", "col"), None))
    return jax.shard_map(
        on_device, mesh=mesh, in_specs=in_specs, out_specs=out_specs, check_vma=False
    )
```

profile of v0, /device:TPU:1, one launch (start us, length us, event | category | flops | bytes accessed | tf_op | source)
XLA Modules:
  0.0 759.6 jit_solution(11323980032133279021)
XLA Ops:
  1.3 4.7 fusion.8
  7.6 5.1 collective-permute-start.1
  14.7 5.0 collective-permute-start.3
  21.6 7.7 %collective-permute-start.5 = (f32[512]{0:T(512)S(1)}, f32[512]{0:T(512)S(1)}, u32[]{:S(2)}, u32[]{:S(2)}) collective-permute-start(f32[512]{0:T(512)S(1)} %bitcast.347), channel_id=1, source_target_pairs={{0,7},{1,8},{2,9},{3,10},{4,11},{5,12},{6,13},{7,14},{8,15},{9,16}... | collective-permute-start | bytes 6152 | tf_op jit(solution)/shard_map/ppermute | solution.py:26
  29.4 5.0 collective-permute-start.6
  36.4 6.2 collective-permute-start.10
  42.6 5.2 collective-permute-start.11
  53.0 5.2 collective-permute-start.8
  58.2 3.9 collective-permute-start.9
  67.3 6.2 fusion.6
  81.3 4.4 collective-permute-start.19
  87.7 9.0 %collective-permute-start.21 = (f32[512]{0:T(512)S(1)}, f32[512]{0:T(512)S(1)}, u32[]{:S(2)}, u32[]{:S(2)}) collective-permute-start(f32[512]{0:T(512)S(1)} %bitcast.355), channel_id=1, source_target_pairs={{0,7},{1,8},{2,9},{3,10},{4,11},{5,12},{6,13},{7,14},{8,15},{9,16}... | collective-permute-start | bytes 6152 | tf_op jit(solution)/shard_map/ppermute | solution.py:26
  96.7 3.7 collective-permute-start.22
  104.6 91.9 %all-reduce = (f32[]{:T(128)}, f32[]{:T(128)}) all-reduce(f32[]{:T(128)} %get-tuple-element.3, f32[]{:T(128)} %get-tuple-element.2), channel_id=1, replica_groups=mesh['row'=32,'col'=8] {'row','col'}, use_global_device_ids=true, to_apply=%region_1.2 | all-reduce | flops 2 | bytes 16 | tf_op jit(solution)/shard_map/psum | solution.py:141
  198.5 74.3 %psum.30 = f32[]{:T(128)} all-reduce(f32[]{:T(128)} %multiply_reduce_fusion.1), channel_id=1, replica_groups=mesh['row'=32,'col'=8] {'row','col'}, use_global_device_ids=true, to_apply=%region_5.6 | all-reduce | flops 1 | bytes 8 | tf_op jit(solution)/shard_map/psum | solution.py:141
  276.9 3.9 collective-permute-start.27
  280.8 2.9 collective-permute-start.28
  287.1 5.4 collective-permute-start.25
  294.5 3.5 collective-permute-start.24
  298.9 6.1 fusion.2
  305.0 4.7 fusion
  315.2 4.7 collective-permute-start.35
  321.8 8.8 %collective-permute-start.37 = (f32[512]{0:T(512)S(1)}, f32[512]{0:T(512)S(1)}, u32[]{:S(2)}, u32[]{:S(2)}) collective-permute-start(f32[512]{0:T(512)S(1)} %bitcast.354), channel_id=1, source_target_pairs={{0,7},{1,8},{2,9},{3,10},{4,11},{5,12},{6,13},{7,14},{8,15},{9,16}... | collective-permute-start | bytes 6152 | tf_op jit(solution)/shard_map/ppermute | solution.py:26
  330.7 4.2 collective-permute-start.38
  334.8 3.4 collective-permute-start.39
  339.6 86.3 %psum.31 = f32[]{:T(128)} all-reduce(f32[]{:T(128)} %multiply_reduce_fusion), channel_id=1, replica_groups=mesh['row'=32,'col'=8] {'row','col'}, use_global_device_ids=true, to_apply=%region_7.8 | all-reduce | flops 1 | bytes 8 | tf_op jit(solution)/shard_map/psum | solution.py:187
  427.2 3.7 collective-permute-start.42
  433.1 4.6 collective-permute-start.44
  441.0 4.6 collective-permute-start.41
  447.5 4.2 collective-permute-start.40
  455.8 16.3 %all-to-all-start = ((f32[3,512,128]{2,0,1:T(4,128)}), f32[3,512,128]{2,0,1:T(4,128)S(1)}, u32[]{:S(2)}, u32[]{:S(2)}) async-start(f32[3,512,128]{2,0,1:T(4,128)} %copy.161), calls=%async_computation | async-start | bytes 2097152 | tf_op jit(solution)/shard_map/all_to_all | solution.py:202
  472.2 16.7 %all-to-all-done = f32[3,512,128]{2,0,1:T(4,128)S(1)} async-done(((f32[3,512,128]{2,0,1:T(4,128)}), f32[3,512,128]{2,0,1:T(4,128)S(1)}, u32[]{:S(2)}, u32[]{:S(2)}) %all-to-all-start) | async-done | bytes 786464 | tf_op jit(solution)/shard_map/all_to_all | solution.py:202
  501.8 3.7 fusion.12
  511.6 12.5 %copy.169 = f32[2,3,16,4096]{2,0,1,3:T(2,128)} copy(f32[2,3,16,4096]{3,2,1,0:T(8,128)S(1)} %pad_maximum_fusion) | data formatting | bytes 3145728 | tf_op jit(solution)/shard_map/stack | solution.py:205
  524.2 19.0 %reshape.239 = f32[32,1,12288]{2,1,0:T(1,128)S(1)} reshape(f32[4096,3,2,16]{3,2,1,0:T(2,128)} %bitcast.279) | data formatting | bytes 3145728
  543.2 26.6 %all_to_all.87 = f32[32,1,12288]{2,1,0:T(1,128)S(1)} all-to-all(f32[32,1,12288]{2,1,0:T(1,128)S(1)} %reshape.239), channel_id=1, replica_groups=mesh['row'=32,'col'=8] {'row'}, dimensions={0} | all-to-all | bytes 3145728 | tf_op jit(solution)/shard_map/all_to_all | solution.py:207
  570.3 4.4 reduce
  574.7 18.7 %reshape.240 = f32[4096,3,2,16]{3,2,1,0:T(2,128)} reshape(f32[32,12288]{1,0:T(8,128)S(1)} %reduce) | data formatting | bytes 3145728
  593.3 14.3 %copy.210 = f32[2,3,16,32,128]{4,2,3,1,0:T(8,128)S(1)} copy(f32[2,3,16,32,128]{2,0,1,4,3:T(2,128)} %bitcast.280) | data formatting | bytes 3145728 | tf_op jit(solution)/shard_map/all_to_all | solution.py:207
  609.9 3.8 all-to-all-start.2
  621.2 32.7 %all-to-all-done.2 = f32[2,3,512,128]{2,0,1,3:T(2,128)S(1)} async-done(((f32[2,3,512,128]{2,0,1,3:T(2,128)}), f32[2,3,512,128]{2,0,1,3:T(2,128)S(1)}, u32[]{:S(2)}, u32[]{:S(2)}) %all-to-all-start.2) | async-done | bytes 1572896 | tf_op jit(solution)/shard_map/all_to_all | solution.py:206
  677.9 4.4 copy.187
  682.3 7.6 reshape.241
  689.8 15.2 %all_to_all.88 = f32[32,1,4096]{2,1,0:T(1,128)S(1)} all-to-all(f32[32,1,4096]{2,1,0:T(1,128)S(1)} %reshape.241), channel_id=1, replica_groups=mesh['row'=32,'col'=8] {'row'}, dimensions={0} | all-to-all | bytes 1048576 | tf_op jit(solution)/shard_map/all_to_all | solution.py:235
  706.9 7.0 reshape.242
  713.8 5.1 copy.212
  719.2 20.9 %all_to_all.89 = f32[2,512,128]{1,0,2:T(2,128)S(1)} all-to-all(f32[2,512,128]{1,0,2:T(2,128)S(1)} %copy.190), channel_id=1, replica_groups=mesh['row'=32,'col'=8] {'col'}, dimensions={2} | all-to-all | bytes 1048576 | tf_op jit(solution)/shard_map/all_to_all | solution.py:234
  743.0 4.2 fusion.326
  (220 shorter events, 125.0 us)
Async XLA Ops:
  6.3 15.3 %collective-permute-start = (f32[512]{0:T(512)S(1)}, f32[512]{0:T(512)S(1)}, u32[]{:S(2)}, u32[]{:S(2)}) collective-permute-start(f32[512]{0:T(512)S(1)} %bitcast.367), channel_id=1, source_target_pairs={{9,0},{10,1},{11,2},{12,3},{13,4},{14,5},{15,6},{16,7},{17,8},{18,... | collective-permute-start | bytes 6152 | tf_op jit(solution)/shard_map/ppermute | solution.py:26
  7.6 21.8 %collective-permute-start.1 = (f32[512]{0:T(512)S(1)}, f32[512]{0:T(512)S(1)}, u32[]{:S(2)}, u32[]{:S(2)}) collective-permute-start(f32[512]{0:T(512)S(1)} %bitcast.364), channel_id=1, source_target_pairs={{8,0},{9,1},{10,2},{11,3},{12,4},{13,5},{14,6},{15,7},{16,8},{17,9... | collective-permute-start | bytes 6152 | tf_op jit(solution)/shard_map/ppermute | solution.py:26
  12.7 21.6 %collective-permute-start.2 = (f32[512]{0:T(512)S(1)}, f32[512]{0:T(512)S(1)}, u32[]{:S(2)}, u32[]{:S(2)}) collective-permute-start(f32[512]{0:T(512)S(1)} %bitcast.361), channel_id=1, source_target_pairs={{7,0},{8,1},{9,2},{10,3},{11,4},{12,5},{13,6},{14,7},{15,8},{16,9}... | collective-permute-start | bytes 6152 | tf_op jit(solution)/shard_map/ppermute | solution.py:26
  14.7 21.0 %collective-permute-start.3 = (f32[512]{0:T(512)S(1)}, f32[512]{0:T(512)S(1)}, u32[]{:S(2)}, u32[]{:S(2)}) collective-permute-start(f32[512]{0:T(512)S(1)} %bitcast.349), channel_id=1, source_target_pairs={{1,0},{2,1},{3,2},{4,3},{5,4},{6,5},{7,6},{8,7},{9,8},{10,9},{11,1... | collective-permute-start | bytes 6152 | tf_op jit(solution)/shard_map/ppermute | solution.py:26
  19.7 16.0 %collective-permute-start.4 = (f32[512]{0:T(512)S(1)}, f32[512]{0:T(512)S(1)}, u32[]{:S(2)}, u32[]{:S(2)}) collective-permute-start(f32[512]{0:T(512)S(1)} %bitcast.348), channel_id=1, source_target_pairs={{0,1},{1,2},{2,3},{3,4},{4,5},{5,6},{6,7},{7,8},{8,9},{9,10},{10,1... | collective-permute-start | bytes 6152 | tf_op jit(solution)/shard_map/ppermute | solution.py:26
  21.6 14.1 %collective-permute-start.5 = (f32[512]{0:T(512)S(1)}, f32[512]{0:T(512)S(1)}, u32[]{:S(2)}, u32[]{:S(2)}) collective-permute-start(f32[512]{0:T(512)S(1)} %bitcast.347), channel_id=1, source_target_pairs={{0,7},{1,8},{2,9},{3,10},{4,11},{5,12},{6,13},{7,14},{8,15},{9,16}... | collective-permute-start | bytes 6152 | tf_op jit(solution)/shard_map/ppermute | solution.py:26
  29.4 6.3 collective-permute-start.6
  36.4 16.6 %collective-permute-start.10 = (f32[512]{0:T(512)S(1)}, f32[512]{0:T(512)S(1)}, u32[]{:S(2)}, u32[]{:S(2)}) collective-permute-start(f32[512]{0:T(512)S(1)} %select_add_fusion.1), channel_id=1, source_target_pairs={{0,7},{1,8},{2,9},{3,10},{4,11},{5,12},{6,13},{7,14},{8,15},{9,16}... | collective-permute-start | bytes 6152 | tf_op jit(solution)/shard_map/ppermute | solution.py:26
  42.6 15.6 %collective-permute-start.11 = (f32[512]{0:T(512)S(1)}, f32[512]{0:T(512)S(1)}, u32[]{:S(2)}, u32[]{:S(2)}) collective-permute-start(f32[512]{0:T(512)S(1)} %select_add_fusion.1), channel_id=1, source_target_pairs={{0,1},{1,2},{2,3},{3,4},{4,5},{5,6},{6,7},{7,8},{8,9},{9,10},{10,1... | collective-permute-start | bytes 6152 | tf_op jit(solution)/shard_map/ppermute | solution.py:26
  47.8 14.3 %collective-permute-start.12 = (f32[512]{0:T(512)S(1)}, f32[512]{0:T(512)S(1)}, u32[]{:S(2)}, u32[]{:S(2)}) collective-permute-start(f32[512]{0:T(512)S(1)} %select_add_fusion.1), channel_id=1, source_target_pairs={{1,0},{2,1},{3,2},{4,3},{5,4},{6,5},{7,6},{8,7},{9,8},{10,9},{11,1... | collective-permute-start | bytes 6152 | tf_op jit(solution)/shard_map/ppermute | solution.py:26
  49.7 14.3 %collective-permute-start.13 = (f32[512]{0:T(512)S(1)}, f32[512]{0:T(512)S(1)}, u32[]{:S(2)}, u32[]{:S(2)}) collective-permute-start(f32[512]{0:T(512)S(1)} %select_add_fusion.1), channel_id=1, source_target_pairs={{7,0},{8,1},{9,2},{10,3},{11,4},{12,5},{13,6},{14,7},{15,8},{16,9}... | collective-permute-start | bytes 6152 | tf_op jit(solution)/shard_map/ppermute | solution.py:26
  51.7 12.4 %collective-permute-start.15 = (f32[512]{0:T(512)S(1)}, f32[512]{0:T(512)S(1)}, u32[]{:S(2)}, u32[]{:S(2)}) collective-permute-start(f32[512]{0:T(512)S(1)} %select_add_fusion.1), channel_id=1, source_target_pairs={{9,0},{10,1},{11,2},{12,3},{13,4},{14,5},{15,6},{16,7},{17,8},{18,... | collective-permute-start | bytes 6152 | tf_op jit(solution)/shard_map/ppermute | solution.py:26
  53.0 11.1 %collective-permute-start.8 = (f32[512]{0:T(512)S(1)}, f32[512]{0:T(512)S(1)}, u32[]{:S(2)}, u32[]{:S(2)}) collective-permute-start(f32[512]{0:T(512)S(1)} %select_add_fusion.1), channel_id=1, source_target_pairs={{0,9},{1,10},{2,11},{3,12},{4,13},{5,14},{6,15},{7,16},{8,17},{9,1... | collective-permute-start | bytes 6152 | tf_op jit(solution)/shard_map/ppermute | solution.py:26
  58.2 6.0 collective-permute-start.9
  62.1 4.9 collective-permute-start.14
  76.2 11.5 %collective-permute-start.16 = (f32[512]{0:T(512)S(1)}, f32[512]{0:T(512)S(1)}, u32[]{:S(2)}, u32[]{:S(2)}) collective-permute-start(f32[512]{0:T(512)S(1)} %bitcast.368), channel_id=1, source_target_pairs={{9,0},{10,1},{11,2},{12,3},{13,4},{14,5},{15,6},{16,7},{17,8},{18,... | collective-permute-start | bytes 6152 | tf_op jit(solution)/shard_map/ppermute | solution.py:26
  77.5 19.2 %collective-permute-start.17 = (f32[512]{0:T(512)S(1)}, f32[512]{0:T(512)S(1)}, u32[]{:S(2)}, u32[]{:S(2)}) collective-permute-start(f32[512]{0:T(512)S(1)} %bitcast.365), channel_id=1, source_target_pairs={{8,0},{9,1},{10,2},{11,3},{12,4},{13,5},{14,6},{15,7},{16,8},{17,9... | collective-permute-start | bytes 6152 | tf_op jit(solution)/shard_map/ppermute | solution.py:26
  79.4 21.0 %collective-permute-start.18 = (f32[512]{0:T(512)S(1)}, f32[512]{0:T(512)S(1)}, u32[]{:S(2)}, u32[]{:S(2)}) collective-permute-start(f32[512]{0:T(512)S(1)} %bitcast.362), channel_id=1, source_target_pairs={{7,0},{8,1},{9,2},{10,3},{11,4},{12,5},{13,6},{14,7},{15,8},{16,9}... | collective-permute-start | bytes 6152 | tf_op jit(solution)/shard_map/ppermute | solution.py:26
  81.3 22.6 %collective-permute-start.19 = (f32[512]{0:T(512)S(1)}, f32[512]{0:T(512)S(1)}, u32[]{:S(2)}, u32[]{:S(2)}) collective-permute-start(f32[512]{0:T(512)S(1)} %bitcast.359), channel_id=1, source_target_pairs={{1,0},{2,1},{3,2},{4,3},{5,4},{6,5},{7,6},{8,7},{9,8},{10,9},{11,1... | collective-permute-start | bytes 6152 | tf_op jit(solution)/shard_map/ppermute | solution.py:26
  85.8 18.2 %collective-permute-start.20 = (f32[512]{0:T(512)S(1)}, f32[512]{0:T(512)S(1)}, u32[]{:S(2)}, u32[]{:S(2)}) collective-permute-start(f32[512]{0:T(512)S(1)} %bitcast.357), channel_id=1, source_target_pairs={{0,1},{1,2},{2,3},{3,4},{4,5},{5,6},{6,7},{7,8},{8,9},{9,10},{10,1... | collective-permute-start | bytes 6152 | tf_op jit(solution)/shard_map/ppermute | solution.py:26
  87.7 16.2 %collective-permute-start.21 = (f32[512]{0:T(512)S(1)}, f32[512]{0:T(512)S(1)}, u32[]{:S(2)}, u32[]{:S(2)}) collective-permute-start(f32[512]{0:T(512)S(1)} %bitcast.355), channel_id=1, source_target_pairs={{0,7},{1,8},{2,9},{3,10},{4,11},{5,12},{6,13},{7,14},{8,15},{9,16}... | collective-permute-start | bytes 6152 | tf_op jit(solution)/shard_map/ppermute | solution.py:26
  96.7 7.3 collective-permute-start.22
  274.2 12.9 %collective-permute-start.26 = (f32[512]{0:T(512)S(1)}, f32[512]{0:T(512)S(1)}, u32[]{:S(2)}, u32[]{:S(2)}) collective-permute-start(f32[512]{0:T(512)S(1)} %multiply_add_fusion.12), channel_id=1, source_target_pairs={{0,7},{1,8},{2,9},{3,10},{4,11},{5,12},{6,13},{7,14},{8,15},{9,16}... | collective-permute-start | bytes 6152 | tf_op jit(solution)/shard_map/ppermute | solution.py:26
  276.9 15.6 %collective-permute-start.27 = (f32[512]{0:T(512)S(1)}, f32[512]{0:T(512)S(1)}, u32[]{:S(2)}, u32[]{:S(2)}) collective-permute-start(f32[512]{0:T(512)S(1)} %multiply_add_fusion.12), channel_id=1, source_target_pairs={{0,1},{1,2},{2,3},{3,4},{4,5},{5,6},{6,7},{7,8},{8,9},{9,10},{10,1... | collective-permute-start | bytes 6152 | tf_op jit(solution)/shard_map/ppermute | solution.py:26
  280.8 13.7 %collective-permute-start.28 = (f32[512]{0:T(512)S(1)}, f32[512]{0:T(512)S(1)}, u32[]{:S(2)}, u32[]{:S(2)}) collective-permute-start(f32[512]{0:T(512)S(1)} %multiply_add_fusion.12), channel_id=1, source_target_pairs={{1,0},{2,1},{3,2},{4,3},{5,4},{6,5},{7,6},{8,7},{9,8},{10,9},{11,1... | collective-permute-start | bytes 6152 | tf_op jit(solution)/shard_map/ppermute | solution.py:26
  283.7 14.3 %collective-permute-start.29 = (f32[512]{0:T(512)S(1)}, f32[512]{0:T(512)S(1)}, u32[]{:S(2)}, u32[]{:S(2)}) collective-permute-start(f32[512]{0:T(512)S(1)} %multiply_add_fusion.12), channel_id=1, source_target_pairs={{7,0},{8,1},{9,2},{10,3},{11,4},{12,5},{13,6},{14,7},{15,8},{16,9}... | collective-permute-start | bytes 6152 | tf_op jit(solution)/shard_map/ppermute | solution.py:26
  285.6 12.3 %collective-permute-start.31 = (f32[512]{0:T(512)S(1)}, f32[512]{0:T(512)S(1)}, u32[]{:S(2)}, u32[]{:S(2)}) collective-permute-start(f32[512]{0:T(512)S(1)} %multiply_add_fusion.12), channel_id=1, source_target_pairs={{9,0},{10,1},{11,2},{12,3},{13,4},{14,5},{15,6},{16,7},{17,8},{18,... | collective-permute-start | bytes 6152 | tf_op jit(solution)/shard_map/ppermute | solution.py:26
  287.1 10.9 %collective-permute-start.25 = (f32[512]{0:T(512)S(1)}, f32[512]{0:T(512)S(1)}, u32[]{:S(2)}, u32[]{:S(2)}) collective-permute-start(f32[512]{0:T(512)S(1)} %multiply_add_fusion.12), channel_id=1, source_target_pairs={{0,8},{1,9},{2,10},{3,11},{4,12},{5,13},{6,14},{7,15},{8,16},{9,17... | collective-permute-start | bytes 6152 | tf_op jit(solution)/shard_map/ppermute | solution.py:26
  292.5 5.5 collective-permute-start.30
  294.5 4.2 collective-permute-start.24
  310.0 11.8 %collective-permute-start.32 = (f32[512]{0:T(512)S(1)}, f32[512]{0:T(512)S(1)}, u32[]{:S(2)}, u32[]{:S(2)}) collective-permute-start(f32[512]{0:T(512)S(1)} %bitcast.366), channel_id=1, source_target_pairs={{9,0},{10,1},{11,2},{12,3},{13,4},{14,5},{15,6},{16,7},{17,8},{18,... | collective-permute-start | bytes 6152 | tf_op jit(solution)/shard_map/ppermute | solution.py:26
  311.3 19.3 %collective-permute-start.33 = (f32[512]{0:T(512)S(1)}, f32[512]{0:T(512)S(1)}, u32[]{:S(2)}, u32[]{:S(2)}) collective-permute-start(f32[512]{0:T(512)S(1)} %bitcast.363), channel_id=1, source_target_pairs={{8,0},{9,1},{10,2},{11,3},{12,4},{13,5},{14,6},{15,7},{16,8},{17,9... | collective-permute-start | bytes 6152 | tf_op jit(solution)/shard_map/ppermute | solution.py:26
  313.2 21.6 %collective-permute-start.34 = (f32[512]{0:T(512)S(1)}, f32[512]{0:T(512)S(1)}, u32[]{:S(2)}, u32[]{:S(2)}) collective-permute-start(f32[512]{0:T(512)S(1)} %bitcast.360), channel_id=1, source_target_pairs={{7,0},{8,1},{9,2},{10,3},{11,4},{12,5},{13,6},{14,7},{15,8},{16,9}... | collective-permute-start | bytes 6152 | tf_op jit(solution)/shard_map/ppermute | solution.py:26
  315.2 23.1 %collective-permute-start.35 = (f32[512]{0:T(512)S(1)}, f32[512]{0:T(512)S(1)}, u32[]{:S(2)}, u32[]{:S(2)}) collective-permute-start(f32[512]{0:T(512)S(1)} %bitcast.358), channel_id=1, source_target_pairs={{1,0},{2,1},{3,2},{4,3},{5,4},{6,5},{7,6},{8,7},{9,8},{10,9},{11,1... | collective-permute-start | bytes 6152 | tf_op jit(solution)/shard_map/ppermute | solution.py:26
  319.9 18.4 %collective-permute-start.36 = (f32[512]{0:T(512)S(1)}, f32[512]{0:T(512)S(1)}, u32[]{:S(2)}, u32[]{:S(2)}) collective-permute-start(f32[512]{0:T(512)S(1)} %bitcast.356), channel_id=1, source_target_pairs={{0,1},{1,2},{2,3},{3,4},{4,5},{5,6},{6,7},{7,8},{8,9},{9,10},{10,1... | collective-permute-start | bytes 6152 | tf_op jit(solution)/shard_map/ppermute | solution.py:26
  321.8 16.5 %collective-permute-start.37 = (f32[512]{0:T(512)S(1)}, f32[512]{0:T(512)S(1)}, u32[]{:S(2)}, u32[]{:S(2)}) collective-permute-start(f32[512]{0:T(512)S(1)} %bitcast.354), channel_id=1, source_target_pairs={{0,7},{1,8},{2,9},{3,10},{4,11},{5,12},{6,13},{7,14},{8,15},{9,16}... | collective-permute-start | bytes 6152 | tf_op jit(solution)/shard_map/ppermute | solution.py:26
  330.7 7.7 %collective-permute-start.38 = (f32[512]{0:T(512)S(1)}, f32[512]{0:T(512)S(1)}, u32[]{:S(2)}, u32[]{:S(2)}) collective-permute-start(f32[512]{0:T(512)S(1)} %bitcast.352), channel_id=1, source_target_pairs={{0,8},{1,9},{2,10},{3,11},{4,12},{5,13},{6,14},{7,15},{8,16},{9,17... | collective-permute-start | bytes 6152 | tf_op jit(solution)/shard_map/ppermute | solution.py:26
  334.8 4.1 collective-permute-start.39
  427.2 13.7 %collective-permute-start.42 = (f32[512]{0:T(512)S(1)}, f32[512]{0:T(512)S(1)}, u32[]{:S(2)}, u32[]{:S(2)}) collective-permute-start(f32[512]{0:T(512)S(1)} %multiply_add_fusion.11), channel_id=1, source_target_pairs={{0,7},{1,8},{2,9},{3,10},{4,11},{5,12},{6,13},{7,14},{8,15},{9,16}... | collective-permute-start | bytes 6152 | tf_op jit(solution)/shard_map/ppermute | solution.py:26
  430.9 14.7 %collective-permute-start.43 = (f32[512]{0:T(512)S(1)}, f32[512]{0:T(512)S(1)}, u32[]{:S(2)}, u32[]{:S(2)}) collective-permute-start(f32[512]{0:T(512)S(1)} %multiply_add_fusion.11), channel_id=1, source_target_pairs={{0,1},{1,2},{2,3},{3,4},{4,5},{5,6},{6,7},{7,8},{8,9},{9,10},{10,1... | collective-permute-start | bytes 6152 | tf_op jit(solution)/shard_map/ppermute | solution.py:26
  433.1 14.4 %collective-permute-start.44 = (f32[512]{0:T(512)S(1)}, f32[512]{0:T(512)S(1)}, u32[]{:S(2)}, u32[]{:S(2)}) collective-permute-start(f32[512]{0:T(512)S(1)} %multiply_add_fusion.11), channel_id=1, source_target_pairs={{1,0},{2,1},{3,2},{4,3},{5,4},{6,5},{7,6},{8,7},{9,8},{10,9},{11,1... | collective-permute-start | bytes 6152 | tf_op jit(solution)/shard_map/ppermute | solution.py:26
  437.7 14.1 %collective-permute-start.45 = (f32[512]{0:T(512)S(1)}, f32[512]{0:T(512)S(1)}, u32[]{:S(2)}, u32[]{:S(2)}) collective-permute-start(f32[512]{0:T(512)S(1)} %multiply_add_fusion.11), channel_id=1, source_target_pairs={{7,0},{8,1},{9,2},{10,3},{11,4},{12,5},{13,6},{14,7},{15,8},{16,9}... | collective-permute-start | bytes 6152 | tf_op jit(solution)/shard_map/ppermute | solution.py:26
  439.7 12.1 %collective-permute-start.47 = (f32[512]{0:T(512)S(1)}, f32[512]{0:T(512)S(1)}, u32[]{:S(2)}, u32[]{:S(2)}) collective-permute-start(f32[512]{0:T(512)S(1)} %multiply_add_fusion.11), channel_id=1, source_target_pairs={{9,0},{10,1},{11,2},{12,3},{13,4},{14,5},{15,6},{16,7},{17,8},{18,... | collective-permute-start | bytes 6152 | tf_op jit(solution)/shard_map/ppermute | solution.py:26
  441.0 10.9 %collective-permute-start.41 = (f32[512]{0:T(512)S(1)}, f32[512]{0:T(512)S(1)}, u32[]{:S(2)}, u32[]{:S(2)}) collective-permute-start(f32[512]{0:T(512)S(1)} %multiply_add_fusion.11), channel_id=1, source_target_pairs={{0,8},{1,9},{2,10},{3,11},{4,12},{5,13},{6,14},{7,15},{8,16},{9,17... | collective-permute-start | bytes 6152 | tf_op jit(solution)/shard_map/ppermute | solution.py:26
  445.6 6.2 collective-permute-start.46
  447.5 4.9 collective-permute-start.40
  455.8 33.1 %all-to-all-start = ((f32[3,512,128]{2,0,1:T(4,128)}), f32[3,512,128]{2,0,1:T(4,128)S(1)}, u32[]{:S(2)}, u32[]{:S(2)}) async-start(f32[3,512,128]{2,0,1:T(4,128)} %copy.161), calls=%async_computation | async-start | bytes 2097152 | tf_op jit(solution)/shard_map/all_to_all | solution.py:202
  609.9 44.0 %all-to-all-start.2 = ((f32[2,3,512,128]{2,0,1,3:T(2,128)}), f32[2,3,512,128]{2,0,1,3:T(2,128)S(1)}, u32[]{:S(2)}, u32[]{:S(2)}) async-start(f32[2,3,512,128]{2,0,1,3:T(2,128)} %copy.172), calls=%async_computation.2 | async-start | bytes 3145728 | tf_op jit(solution)/shard_map/all_to_all | solution.py:206
  (10 other events, 259.2 us)
where the time goes:
time: 771 us; the launch traced here: 760 us
  blocking collectives  315 us (41%)
  starting transfers between devices  180 us (23%)
  local copies, waits for them, and re-layouts  123 us (16%)
  matrix products  61.8 us (8%)
  waiting for transfers between devices  55 us (7%)
  between operations  13.2 us (2%)
  other arithmetic  11.7 us (2%)
    psum x2, blocking collectives, squares(): return lax.psum(jnp.sum(residual * residual), ('row', 'col'))  166 us
    ppermute x48, starting transfers between devices, shifted(): return lax.ppermute(x, axis, pairs)  160 us
    psum x1, blocking collectives, on_device(): lax.psum(jnp.sum(direction * applied), ('row', 'col'))  86.3 us
    unnamed x22, local copies, waits for them, and re-layouts  52.5 us
    all_to_all x1, waiting for transfers between devices, on_device(): lax.all_to_all(lax.all_to_all(spectra, 'row', split_axis=3, concat_axis=2...  32.7 us
    all_to_all x1, blocking collectives, on_device(): lax.all_to_all(spectra, 'row', split_axis=3, concat_axis=2, tiled=True)  26.6 us
    all_to_all x1, blocking collectives, on_device(): lax.all_to_all(lax.all_to_all(stacked, 'row', split_axis=2, concat_axis=1...  20.9 us
    another operation x3, local copies, waits for them, and re-layouts, on_device(): spectra = jnp.stack([north_real, north_imag])  17.2 us
  transfers between devices with their start and end apart: 50, of which 7 were waited for; matrix products, arithmetic and copies ran while one was open for 0% of the time, Pallas kernels for 0%

commit v1 on v0

v1 whole, which is shorter than its diff:
```python
import functools
import math

import jax
import jax.numpy as jnp
import ml_dtypes
import numpy as np
from jax import lax
from jax.experimental import pallas as pl
from jax.experimental.pallas import tpu as pltpu
from jax.sharding import PartitionSpec as P

F32 = jnp.float32
BF16 = jnp.bfloat16
MESH = pl.DeviceIdType.MESH
ROWS, COLS = 32, 8
FULL = 4096
REFINE = 16
SLOTS = 256
OFFSETS = tuple((a, b) for a in (-1, 0, 1) for b in (-1, 0, 1))
SCALE = 1.0 / 16777216.0

(T1, T2A, T2B, TWIN, T3P, T3Q, ZP, RP, ZQ, RQ, Z1, R1, Z2, R2) = range(14)
PHASES = 14
RETURN0, COLLECT0, RETURN1, COLLECT1 = range(4)


def halves(x):
    high = x.astype(np.float32).astype(ml_dtypes.bfloat16)
    low = (x - high.astype(np.float64)).astype(np.float32).astype(ml_dtypes.bfloat16)
    return np.stack([high, low])


@functools.lru_cache(maxsize=None)
def tables():
    two_pi = 2.0 * math.pi
    a = np.arange(32)
    ka = np.arange(16)
    n = np.arange(128)
    kn = np.arange(128)
    ang_a = two_pi * np.outer(ka, a) / 32
    outer = np.stack([np.cos(ang_a), -np.sin(ang_a)])
    outer[1, 0] = (-1.0) ** a
    eye = np.eye(16)
    outer_fwd = np.kron(outer.reshape(32, 32), eye)
    inv = np.stack([2 * np.cos(ang_a), -2 * np.sin(ang_a)])
    inv[0, 0] = 1.0
    inv[1, 0] = (-1.0) ** a
    outer_inv = np.kron(inv.reshape(32, 32).T, eye)
    ang_t = two_pi * np.outer(ka, n) / 4096
    twist = np.stack([np.cos(ang_t), np.sin(ang_t)])[:, :, None, :]
    th = two_pi * np.outer(n, kn) / 128
    c, s = np.cos(th), np.sin(th)
    inner_fwd = np.block([[c, -s], [s, c]])
    inner_inv = np.block([[c, s], [-s, c]]).T
    inner_inv = np.block([[c.T, s.T], [-s.T, c.T]])
    k0 = np.arange(64)
    th0 = two_pi * np.outer(n, 32 * k0) / 4096
    th1 = two_pi * np.outer(n, 16 + 32 * k0) / 4096
    alt = (-1.0) ** n
    first_fwd = np.zeros((256, 256))
    first_fwd[:128, 0:64] = np.cos(th0)
    first_fwd[:128, 128:192] = -np.sin(th0)
    first_fwd[:128, 128] = alt
    first_fwd[128:, 64:128] = np.cos(th1)
    first_fwd[128:, 192:256] = -np.sin(th1)
    first_inv = np.zeros((256, 256))
    first_inv[0:64, :128] = 2 * np.cos(th0).T
    first_inv[0, :128] = 1.0
    first_inv[128:192, :128] = -2 * np.sin(th0).T
    first_inv[128, :128] = alt
    first_inv[64:128, 128:] = 2 * np.cos(th1).T
    first_inv[192:256, 128:] = -2 * np.sin(th1).T
    w = np.arange(512)
    th_w = two_pi * (np.outer(w, w) % 512) / 512
    east = np.concatenate([np.cos(th_w), np.sin(th_w)])
    kb = np.arange(8)
    ang_c = two_pi * np.outer(np.arange(32), 16 * kb) / 4096
    twist_coarse = np.concatenate([np.cos(ang_c), np.sin(ang_c)], axis=1)
    ang_f = two_pi * np.outer(kb, np.arange(16)) / 4096
    twist_fine = np.broadcast_to(
        np.stack([np.cos(ang_f), np.sin(ang_f)])[..., None], (2, 8, 16, 128)
    )
    u = np.arange(4096)
    g = np.arange(256)
    hat = np.maximum(0.0, 1.0 - np.abs((u[:, None] + 0.5) / REFINE - 0.5 - g[None, :]))
    spec = np.fft.fft(hat, axis=0)
    east_hat = np.stack(
        [np.concatenate([spec[k::8].real, spec[k::8].imag]) for k in range(8)]
    )
    order = np.array(
        [8 * i + 4 * m2 + g4 for i in range(32) for g4 in range(4) for m2 in range(2)]
    )
    north_hat = np.zeros((32, 144, 256))
    lane = np.arange(64)
    for col in range(8):
        for ka1 in range(2):
            for knh in range(2):
                slot = 2 * col + ka1
                ku = slot + 32 * (64 * knh + lane) if slot else 16 * knh + 32 * lane
                idx = col * 4 + ka1 * 2 + knh
                north_hat[idx, :64] = spec[ku].real[:, order]
                north_hat[idx, 64:128] = spec[ku].imag[:, order]
    north_hat[0, 128] = spec[2048].real[order]
    f32 = np.float32
    return dict(
        outer_fwd=halves(outer_fwd),
        outer_inv=halves(outer_inv),
        inner_fwd=halves(inner_fwd),
        inner_inv=halves(inner_inv),
        first_fwd=halves(first_fwd),
        first_inv=halves(first_inv),
        east=halves(east),
        twist=twist.astype(f32),
        twist_fine=np.ascontiguousarray(twist_fine).astype(f32),
        twist_coarse=twist_coarse.astype(f32),
        east_hat=np.ascontiguousarray(halves(east_hat).swapaxes(0, 1)),
        north_hat=np.ascontiguousarray(halves(north_hat).swapaxes(0, 1)),
    )


TABLE_NAMES = (
    "outer_fwd",
    "inner_fwd",
    "first_fwd",
    "twist",
    "twist_fine",
    "east",
    "north_hat",
    "east_hat",
    "inner_inv",
    "first_inv",
    "outer_inv",
)


def split(x):
    high = x.astype(BF16)
    return high, (x - high.astype(F32)).astype(BF16)


def dot3(lhs, rhs, transposed=False):
    dims = (((1,), (1 if transposed else 0,)), ((), ()))

    def one(x, y):
        return lax.dot_general(x, y, dims, preferred_element_type=F32)

    return one(lhs[0], rhs[0]) + (one(lhs[0], rhs[1]) + one(lhs[1], rhs[0]))


def short_transform(values, sign):
    count = len(values)
    if count == 1:
        return values
    even = short_transform(values[0::2], sign)
    odd = short_transform(values[1::2], sign)
    out = [None] * count
    for k in range(count // 2):
        re, im = odd[k]
        if k == 0:
            pass
        elif 4 * k == count:
            re, im = -sign * im, sign * re
        else:
            co = math.cos(2 * math.pi * k / count)
            si = sign * math.sin(2 * math.pi * k / count)
            re, im = re * co - im * si, re * si + im * co
        ere, eim = even[k]
        out[k] = (ere + re, eim + im)
        out[k + count // 2] = (ere - re, eim - im)
    return out


def pole_of(fn, fe, angles):
    radius = jnp.sqrt(fn * fn + fe * fe)
    safe = jnp.where(radius > 0.0, radius, 1.0)
    nn = jnp.where(radius > 0.0, fn / safe, 0.0)
    ne = jnp.where(radius > 0.0, fe / safe, 0.0)
    re = im = None
    for m in range(2):
        vertical = angles[m]
        horizontal = angles[2 + m]
        along = horizontal * (angles[4 + m] * nn + angles[6 + m] * ne)
        inverse = 1.0 / (vertical * vertical + along * along)
        one_re, one_im = vertical * inverse, -along * inverse
        if re is None:
            re, im = one_re, one_im
        else:
            re, im = re * one_re - im * one_im, re * one_im + im * one_re
    return re, im, radius


def lanes_of(shape):
    return lax.broadcasted_iota(jnp.int32, shape, len(shape) - 1)


def signs_of(shape):
    return jnp.where(lanes_of(shape) < 64, 1.0, -1.0).astype(F32)


def swap(x):
    return pltpu.roll(x, 64, axis=x.ndim - 1)


def kernel(
    foot, where_code, counts, params, twist_coarse,
    tiles_hbm, readings, grid,
    outer_fwd_h, inner_fwd_h, first_fwd_h, twist_h, twist_fine_h, east_h,
    north_hat_h, east_hat_h, inner_inv_h, first_inv_h, outer_inv_h,
    coef_out, map_out,
    tiles, outer_fwd, inner_fwd, first_fwd, twist, twist_fine, east,
    north_hat, east_hat, inner_inv, first_inv, outer_inv,
    in1, send2, in2, send3, in3, twin_send, twin_in, send4, in4, send5, in5,
    spec_main, spec_twin, filt,
    spread0, spread1, ret0, ret1, halo0, halo1, chosen,
    p_own, q_own, zp, zq, xp_send, xq_send, xp, xq,
    y_p, y_q, sum1, sum2, sum1b, sum2b, z1, r1, z2, r2,
    load_sem, send_sem, recv_sem, halo_send, halo_recv,
):
    r = lax.axis_index("row")
    c = lax.axis_index("col")
    kb = r // 4
    low2 = r % 4
    special = (c == 0) & (low2 == 0)

    loads = [
        (tiles_hbm, tiles),
        (outer_fwd_h, outer_fwd),
        (inner_fwd_h, inner_fwd),
        (first_fwd_h, first_fwd),
        (twist_h, twist),
        (twist_fine_h, twist_fine),
        (east_h, east),
        (north_hat_h.at[c * 4 + low2], north_hat),
        (east_hat_h.at[kb], east_hat),
        (inner_inv_h, inner_inv),
        (first_inv_h, first_inv),
        (outer_inv_h, outer_inv),
    ]
    copies = [
        pltpu.make_async_copy(src, dst, load_sem.at[i]) for i, (src, dst) in enumerate(loads)
    ]
    for one in copies:
        one.start()

    barrier = pltpu.get_barrier_semaphore()

    def greet(row, col):
        pl.semaphore_signal(barrier, inc=1, device_id=(row, col), device_id_type=MESH)

    def exists(a, b):
        return (r + a >= 0) & (r + a < ROWS) & (c + b >= 0) & (c + b < COLS)

    @pl.loop(1, ROWS)
    def _(i):
        greet((r + i) % ROWS, c)

    @pl.loop(1, COLS)
    def _(i):
        greet(r, (c + i) % COLS)

    expected = jnp.int32(ROWS - 1 + COLS - 1)
    for a in (-1, 1):
        for b in (-1, 1):
            there = exists(a, b)
            expected = expected + there.astype(jnp.int32)

            @pl.when(there)
            def _():
                greet(r + a, c + b)

    self_last = kb == c

    @pl.loop(0, COLS)
    def _(i):
        @pl.when(jnp.logical_not(self_last & (i == kb)))
        def _():
            greet(i * 4 + low2, kb)

        @pl.when(jnp.logical_not(self_last & (i == c)))
        def _():
            greet(c * 4 + low2, i)

    expected = expected + 16 - 2 * self_last.astype(jnp.int32)
    pl.semaphore_wait(barrier, expected)

    def push(src, dst, phase, row, col):
        pltpu.make_async_remote_copy(
            src_ref=src, dst_ref=dst, send_sem=send_sem.at[phase], recv_sem=recv_sem.at[phase],
            device_id=(row, col), device_id_type=MESH,
        ).start()

    def keep(src, dst, phase):
        pltpu.make_async_copy(src, dst, recv_sem.at[phase]).start()

    def arrived(dst, phase):
        pltpu.make_async_copy(dst, dst, recv_sem.at[phase]).wait()

    def left(ref, phase):
        pltpu.make_async_copy(ref, ref, send_sem.at[phase]).wait()

    def rows_exchange(src, dst, phase):
        keep(src.at[r], dst.at[r], phase)

        @pl.loop(1, ROWS)
        def _(i):
            row = (r + i) % ROWS
            push(src.at[row], dst.at[r], phase, row, c)

    def cols_exchange(src, dst, phase):
        keep(src.at[c], dst.at[c], phase)

        @pl.loop(1, COLS)
        def _(i):
            col = (c + i) % COLS
            push(src.at[col], dst.at[c], phase, r, col)

    def rows_share(src, dst, phase):
        keep(src, dst.at[r], phase)

        @pl.loop(1, ROWS)
        def _(i):
            push(src, dst.at[r], phase, (r + i) % ROWS, c)

    def cols_share(src, dst, phase):
        keep(src, dst.at[c], phase)

        @pl.loop(1, COLS)
        def _(i):
            push(src, dst.at[c], phase, r, (c + i) % COLS)

    def halo_copy(src, dst, turn, code, row, col):
        return pltpu.make_async_remote_copy(
            src_ref=src, dst_ref=dst,
            send_sem=halo_send.at[turn, code], recv_sem=halo_recv.at[turn, code],
            device_id=(row, col), device_id_type=MESH,
        )

    def return_start(spread, dst, turn):
        for code, (a, b) in enumerate(OFFSETS):
            if code != 4:

                @pl.when(exists(a, b))
                def _():
                    halo_copy(spread.at[code], dst.at[code], turn, code, r + a, c + b).start()

    def collect_start(own, dst, turn):
        for code, (a, b) in enumerate(OFFSETS):
            if code != 4:

                @pl.when(exists(-a, -b))
                def _():
                    halo_copy(own, dst.at[code], turn, code, r - a, c - b).start()

    def halo_wait(src, dst, turn, collecting):
        for code, (a, b) in enumerate(OFFSETS):
            if code != 4:
                away = -1 if collecting else 1
                source = exists(-away * a, -away * b)

                @pl.when(source)
                def _():
                    halo_copy(src, dst.at[code], turn, code, r, c).wait_recv()

                @pl.when(jnp.logical_not(source))
                def _():
                    dst[code] = jnp.zeros((8, 128), F32)

    def halo_left(src, dst, turn, collecting):
        for code, (a, b) in enumerate(OFFSETS):
            if code != 4:
                away = -1 if collecting else 1

                @pl.when(exists(away * a, away * b))
                def _():
                    halo_copy(src, dst.at[code], turn, code, r, c).wait_send()

    sub8 = lax.broadcasted_iota(jnp.int32, (8, 128), 0)

    def spread_of(y, out):
        @pl.loop(0, 9)
        def _(code):
            k = where_code[code]
            total = jnp.zeros((8, 128), F32)
            for m in range(4):
                acc = [jnp.zeros((8, 128), F32) for _ in range(4)]
                for t in range(32):
                    part = tiles[k, pl.ds(8 * t, 8), pl.ds(128 * m, 128)]
                    acc[t % 4] = acc[t % 4] + part * y[pl.ds(8 * t, 8), :]
                row = jnp.sum((acc[0] + acc[1]) + (acc[2] + acc[3]), axis=0, keepdims=True)
                total = total + jnp.where(sub8 == m, jnp.broadcast_to(row, (8, 128)), 0.0)
            out[code] = total

    def readings_of(blocks, y):
        @pl.loop(0, 8)
        def _(chunk):
            base = pl.multiple_of(32 * chunk, 32)
            acc = [jnp.zeros((8, 128), F32) for _ in range(4)]
            for k in range(9):
                code = foot[k]
                for m in range(4):
                    row = jnp.broadcast_to(blocks[code, pl.ds(m, 1), :], (8, 128))
                    for t in range(4):
                        part = tiles[k, pl.ds(base + 8 * t, 8), pl.ds(128 * m, 128)]
                        acc[t] = acc[t] + part * row
            for t in range(4):
                slot = lax.broadcasted_iota(jnp.int32, (8, 128), 0) + (base + 8 * t)
                total = jnp.sum(acc[t], axis=1, keepdims=True)
                y[pl.ds(base + 8 * t, 8), :] = jnp.where(
                    slot < counts[0], jnp.broadcast_to(total, (8, 128)), 0.0
                )

    def gather_blocks(own, halo):
        for code in range(9):
            chosen[code] = own[...] if code == 4 else halo[code]

    def own_sum(spread, ret):
        total = spread[4]
        for code in range(9):
            if code != 4:
                total = total + ret[code]
        return total

    def total_of(x):
        return jnp.sum(jnp.sum(x, axis=1, keepdims=True), axis=0, keepdims=True)

    lane8 = lanes_of((8, 128))

    def pack(parts):
        out = jnp.zeros((8, 128), F32)
        for i, part in enumerate(parts):
            out = out + jnp.where(
                (lane8 == i) & (sub8 == 0), jnp.broadcast_to(part, (8, 128)), 0.0
            )
        return out

    def unpack(x, i):
        return total_of(jnp.where((lane8 == i) & (sub8 == 0), x, 0.0))

    rows_exchange(grid, in1, T1)

    eye = lax.broadcasted_iota(jnp.int32, (SLOTS, SLOTS), 0) == lanes_of((SLOTS, SLOTS))
    column = jnp.sum(
        jnp.where(eye, jnp.broadcast_to(readings[...], (SLOTS, SLOTS)), 0.0),
        axis=1, keepdims=True,
    )
    slot_index = lax.broadcasted_iota(jnp.int32, (SLOTS, 128), 0)
    y_q[...] = jnp.where(slot_index < counts[0], jnp.broadcast_to(column, (SLOTS, 128)), 0.0)
    copies[0].wait()
    spread_of(y_q, spread0)
    return_start(spread0, ret0, RETURN0)

    for i in range(1, 6):
        copies[i].wait()
    arrived(in1, T1)
    outer = dot3(
        (outer_fwd[0], outer_fwd[1]), split(in1[...].reshape(512, 128))
    ).reshape(2, 16, 16, 128)
    tw_c, tw_s = twist[0], twist[1]
    turned = jnp.concatenate(
        [
            (outer[0] * tw_c + outer[1] * tw_s).reshape(256, 128),
            (outer[1] * tw_c - outer[0] * tw_s).reshape(256, 128),
        ],
        axis=1,
    )
    turned_h, turned_l = split(turned)
    send2[...] = dot3((turned_h, turned_l), (inner_fwd[0], inner_fwd[1])).reshape(8, 32, 256)
    send2[0, 0:16, :] = dot3((turned_h[:16], turned_l[:16]), (first_fwd[0], first_fwd[1]))
    cols_exchange(send2, in2, T2A)

    halo_wait(spread0.at[4], ret0, RETURN0, False)
    p_own[...] = own_sum(spread0, ret0)
    collect_start(p_own, halo0, COLLECT0)
    cols_share(p_own, zp, ZP)
    halo_wait(p_own, halo0, COLLECT0, True)
    gather_blocks(p_own, halo0)
    readings_of(chosen, y_p)
    p_val = p_own[...]
    sum1[...] = pack([total_of(y_p[...] * y_p[...]) * (1.0 / 128.0), total_of(p_val * p_val)])
    cols_share(sum1, z1, Z1)
    spread_of(y_p, spread1)
    return_start(spread1, ret1, RETURN1)

    lane_half = lanes_of((8, 128)) // 32

    def coarse_rows(z, out):
        for half in range(2):
            for g in range(4):
                total = jnp.zeros((8, 128), F32)
                for j in range(4):
                    block = z[4 * half + j]
                    shift = (32 * (j - g)) % 128
                    if shift:
                        block = pltpu.roll(block, shift, axis=1)
                    total = jnp.where(lane_half == j, block, total)
                lanes = pl.ds(128 * half, 128)
                out[pl.ds(2 * g, 2), lanes] = total[0:2]
                out[pl.ds(8 + 2 * g, 2), lanes] = total[2:4]

    arrived(zp, ZP)
    coarse_rows(zp, xp_send)
    rows_share(xp_send, xp, RP)

    arrived(in2, T2A)
    pairs = short_transform(
        [(in2[b, :, 0:128], in2[b, :, 128:256]) for b in range(8)], -1.0
    )
    lane32 = lanes_of((32, 128))
    sub32 = lax.broadcasted_iota(jnp.int32, (32, 128), 0)
    apart = (lane32 == 0) & (sub32 < 16) & (c == 0)
    left16 = lanes_of((16, 128)) < 64
    for k in range(8):
        re, im = pairs[k]
        other_re, other_im = pairs[(8 - k) % 8]
        main_re = jnp.where(apart, 0.5 * (re + other_re), re)
        main_im = jnp.where(apart, 0.5 * (im - other_im), im)
        twin_re = 0.5 * (im[:16] + other_im[:16])
        twin_im = 0.5 * (other_re[:16] - re[:16])
        co = twist_coarse[r, k]
        si = twist_coarse[r, 8 + k]
        fine_c, fine_s = twist_fine[0, k], twist_fine[1, k]
        tc = co * fine_c - si * fine_s
        ts = si * fine_c + co * fine_s
        for ka1 in range(2):
            xr, xi = main_re[16 * ka1:16 * ka1 + 16], main_im[16 * ka1:16 * ka1 + 16]
            yr, yi = xr * tc + xi * ts, xi * tc - xr * ts
            send3[4 * k + 2 * ka1] = jnp.where(left16, yr, swap(yi))
            send3[4 * k + 2 * ka1 + 1] = jnp.where(left16, swap(yr), yi)
        yr, yi = twin_re * tc + twin_im * ts, twin_im * tc - twin_re * ts
        twin_send[k] = jnp.where(left16, yr, swap(yi))
    rows_exchange(send3, in3, T2B)

    @pl.when(c == 0)
    def _():
        @pl.loop(0, 8)
        def _(k):
            @pl.when(4 * k == r)
            def _():
                keep(twin_send.at[k], twin_in.at[r], TWIN)

            @pl.when(4 * k != r)
            def _():
                push(twin_send.at[k], twin_in.at[r], TWIN, 4 * k, c)

    halo_wait(spread1.at[4], ret1, RETURN1, False)
    damping = params[0]
    q_own[...] = own_sum(spread1, ret1) + damping * p_own[...]
    collect_start(q_own, halo1, COLLECT1)
    cols_share(q_own, zq, ZQ)

    arrived(z1, Z1)
    half_sum = z1[0]
    for i in range(1, 8):
        half_sum = half_sum + z1[i]
    sum1b[...] = half_sum
    rows_share(sum1b, r1, R1)

    halo_wait(q_own, halo1, COLLECT1, True)
    gather_blocks(q_own, halo1)
    readings_of(chosen, y_q)

    arrived(zq, ZQ)
    coarse_rows(zq, xq_send)
    rows_share(xq_send, xq, RQ)

    arrived(r1, R1)
    full_sum = jnp.sum(r1[...], axis=0)
    g00, rr0 = unpack(full_sum, 0), unpack(full_sum, 1)
    step0 = rr0 / (g00 + damping * rr0)
    p_val = p_own[...]
    resid = p_val - step0 * q_own[...]
    yr1 = y_p[...] - step0 * y_q[...]
    sum2[...] = pack(
        [
            total_of(yr1 * yr1) * (1.0 / 128.0),
            total_of(yr1 * y_p[...]) * (1.0 / 128.0),
            total_of(resid * resid),
            total_of(resid * p_val),
        ]
    )
    cols_share(sum2, z2, Z2)

    knh = low2 % 2
    ka = 2 * c + low2 // 2

    @pl.loop(0, 16)
    def _(chunk):
        base = pl.multiple_of(32 * chunk, 32)
        shape = (32, 128)
        lane = lanes_of(shape)
        kv = kb + 8 * (lax.broadcasted_iota(jnp.int32, shape, 0) + base)
        ku = jnp.where(ka > 0, ka + 32 * (64 * knh + lane), 16 * knh + 32 * lane)
        ku = jnp.where(lane < 64, ku, 2048)
        fe = jnp.where(kv < 2048, kv, kv - 4096).astype(F32) * (1.0 / 4096.0)
        fn = jnp.where(ku < 2048, ku, ku - 4096).astype(F32) * (1.0 / 4096.0)
        angles = [params[3 + i] for i in range(8)]
        re_a, im_a, radius = pole_of(fn, fe, angles)
        re_b, im_b, _ = pole_of(
            jnp.where(ku == 2048, 0.5, fn), jnp.where(kv == 2048, 0.5, fe), angles
        )
        kappa = (2.0 * math.pi) * radius
        made = [
            (0.5 * SCALE) * (re_a + re_b),
            (0.5 * SCALE) * (im_a + im_b),
            jnp.exp(-kappa * params[1]),
            jnp.exp(-kappa * params[2]),
        ]
        for i, one in enumerate(made):
            other = swap(one)
            main = jnp.where(lane < 64, one, other)
            twin = jnp.where(lane < 64, other, one)
            if i == 1:
                sign = signs_of(shape)
                main, twin = main * sign, twin * sign
            filt[i, pl.ds(base, 32), :] = main
            filt[4 + i, pl.ds(base, 32), :] = twin

    copies[6].wait()
    arrived(in3, T2B)

    @pl.when(special)
    def _():
        arrived(twin_in, TWIN)

    @pl.when(jnp.logical_not(special))
    def _():
        twin_in[...] = jnp.zeros((32, 16, 128), F32)

    both = jnp.concatenate(
        [in3[...].reshape(512, 128), twin_in[...].reshape(512, 128)], axis=1
    )
    spun = dot3((east[0], east[1]), split(both))
    sign512 = signs_of((512, 128))
    spec_main[...] = spun[:512, :128] + sign512 * swap(spun[512:, :128])
    spec_twin[...] = spun[:512, 128:] + sign512 * swap(spun[512:, 128:])

    arrived(z2, Z2)
    half_sum = z2[0]
    for i in range(1, 8):
        half_sum = half_sum + z2[i]
    sum2b[...] = half_sum
    rows_share(sum2b, r2, R2)

    arrived(xp, RP)
    arrived(xq, RQ)
    for i in range(7, 12):
        copies[i].wait()
    arrived(r2, R2)
    full_sum = jnp.sum(r2[...], axis=0)
    g11, g10 = unpack(full_sum, 0), unpack(full_sum, 1)
    rr1, r10 = unpack(full_sum, 2), unpack(full_sum, 3)
    beta = rr1 / rr0
    bent = (g11 + 2.0 * beta * g10 + beta * beta * g00) + damping * (
        rr1 + 2.0 * beta * r10 + beta * beta * rr0
    )
    step1 = rr1 / bent
    coef_out[...] = step0 * p_val + step1 * (resid + beta * p_val)

    alpha = step0 + step1 + step1 * beta
    gamma = -step1 * step0
    rows_of = []
    extra = []
    for layer in range(2):
        coarse = alpha * xp[:, 8 * layer:8 * layer + 8, :].reshape(256, 256) + gamma * xq[
            :, 8 * layer:8 * layer + 8, :
        ].reshape(256, 256)
        north = dot3((north_hat[0], north_hat[1]), split(coarse))
        rows_of.append(north[:128])
        extra.append(north[128:144])
    rows_of.extend(extra)
    rows_of.append(jnp.zeros((96, 256), F32))
    model = dot3(
        (east_hat[0], east_hat[1]), split(jnp.concatenate(rows_of, axis=0)), transposed=True
    )
    left512 = lanes_of((512, 128)) < 64
    total = spec_main[...]
    twin = spec_twin[...]
    for layer in range(2):
        lanes = slice(128 * layer, 128 * layer + 128)
        plane = model[:512, lanes] - sign512 * swap(model[512:, lanes])
        total = total + filt[2 + layer] * plane
        top, bottom = model[:512, 256:], model[512:, 256:]
        if layer:
            top = pltpu.roll(top, 112, axis=1)
            bottom = pltpu.roll(bottom, 112, axis=1)
        twin = twin + filt[6 + layer] * jnp.where(left512, top, swap(bottom))
    shaped = filt[0] * total - filt[1] * swap(total)
    shaped_twin = filt[4] * twin - filt[5] * swap(twin)
    joined = special & (lanes_of((512, 128)) % 64 == 0)
    shaped = shaped - jnp.where(joined, sign512 * swap(shaped_twin), 0.0)

    spun = dot3((east[0], east[1]), split(shaped))
    back = spun[:512] - sign512 * swap(spun[512:])
    sign16 = signs_of((16, 128))
    fine_c, fine_s = twist_fine[0, kb], twist_fine[1, kb]
    for chunk in range(32):
        block = back[16 * chunk:16 * chunk + 16]
        co = twist_coarse[chunk, kb]
        si = twist_coarse[chunk, 8 + kb]
        tc = co * fine_c - si * fine_s
        ts = si * fine_c + co * fine_s
        send4[(chunk % 8) * 4 + chunk // 8] = block * tc - sign16 * ts * swap(block)
    rows_exchange(send4, in4, T3P)

    arrived(in4, T3P)
    for ka1 in range(2):
        values = []
        for k in range(8):
            m0, m1 = in4[4 * k + 2 * ka1], in4[4 * k + 2 * ka1 + 1]
            values.append((jnp.where(left16, m0, swap(m1)), jnp.where(left16, swap(m0), m1)))
        for b, (re, im) in enumerate(short_transform(values, 1.0)):
            send5[b, 0, 16 * ka1:16 * ka1 + 16, :] = re
            send5[b, 1, 16 * ka1:16 * ka1 + 16, :] = im

    @pl.loop(0, COLS)
    def _(b):
        mine = self_last & (b == kb)

        @pl.when(mine)
        def _():
            keep(send5.at[b], in5.at[c], T3Q)

        @pl.when(jnp.logical_not(mine))
        def _():
            push(send5.at[b], in5.at[c], T3Q, 4 * b + low2, kb)

    arrived(in5, T3Q)

    pair = jnp.concatenate(
        [in5[:, 0].reshape(256, 128), in5[:, 1].reshape(256, 128)], axis=1
    )
    pair_h, pair_l = split(pair)
    inner = dot3((pair_h, pair_l), (inner_inv[0], inner_inv[1]))
    first = dot3((pair_h[:16], pair_l[:16]), (first_inv[0], first_inv[1]))
    inner = jnp.concatenate([first, inner[16:]], axis=0)
    re, im = inner[:, :128].reshape(16, 16, 128), inner[:, 128:].reshape(16, 16, 128)
    turned = jnp.concatenate(
        [
            (re * tw_c - im * tw_s).reshape(256, 128),
            (im * tw_c + re * tw_s).reshape(256, 128),
        ],
        axis=0,
    )
    final = dot3((outer_inv[0], outer_inv[1]), split(turned))
    for i in range(32):
        map_out[:, pl.ds(128 * i, 128)] = final[16 * i:16 * i + 16]

    for buf, phase in ((in1, T1), (send3, T2B), (send4, T3P), (xp, RP), (xq, RQ), (r1, R1), (r2, R2)):
        left(buf.at[pl.ds(0, ROWS - 1)], phase)
    for buf, phase in ((send2, T2A), (zp, ZP), (zq, ZQ), (z1, Z1), (z2, Z2)):
        left(buf.at[pl.ds(0, COLS - 1)], phase)

    @pl.when(self_last)
    def _():
        left(send5.at[pl.ds(0, COLS - 1)], T3Q)

    @pl.when(jnp.logical_not(self_last))
    def _():
        left(send5, T3Q)

    @pl.when((c == 0) & (low2 == 0))
    def _():
        left(twin_send.at[pl.ds(0, 7)], TWIN)

    @pl.when((c == 0) & (low2 != 0))
    def _():
        left(twin_send, TWIN)

    halo_left(spread0.at[4], ret0, RETURN0, False)
    halo_left(p_own, halo0, COLLECT0, True)
    halo_left(spread1.at[4], ret1, RETURN1, False)
    halo_left(q_own, halo1, COLLECT1, True)


def on_device(
    kernel_tiles, footprints, counts, readings, damping, layer_depth,
    inclinations, declinations, resid_grid,
):
    table = tables()
    foot = footprints.reshape(9)
    nine = jnp.arange(9, dtype=jnp.int32)
    where_code = jnp.sum(jnp.where(foot[:, None] == nine[None, :], nine[:, None], 0), axis=0)
    params = jnp.concatenate(
        [
            damping, layer_depth,
            jnp.sin(inclinations), jnp.cos(inclinations),
            jnp.cos(declinations), jnp.sin(declinations),
        ]
    )
    consts = [jnp.asarray(table[name]) for name in TABLE_NAMES]
    shapes = [x.shape for x in consts]
    shapes[6] = shapes[6][1:]
    shapes[7] = shapes[7][1:]
    kinds = [x.dtype for x in consts]
    smem = pl.BlockSpec(memory_space=pltpu.SMEM)
    vmem = pl.BlockSpec(memory_space=pltpu.VMEM)
    hbm = pl.BlockSpec(memory_space=pl.ANY)

    def v(*shape):
        return pltpu.VMEM(shape, F32)

    block = (32, 16, 128)
    scratch = [v(9, 256, 512)]
    scratch += [pltpu.VMEM(shape, kind) for shape, kind in zip(shapes, kinds)]
    scratch += [
        v(*block), v(8, 32, 256), v(8, 32, 256), v(*block), v(*block),
        v(8, 16, 128), v(*block), v(*block), v(*block), v(8, 2, 32, 128), v(8, 2, 32, 128),
        v(512, 128), v(512, 128), v(8, 512, 128),
    ]
    scratch += [v(9, 8, 128) for _ in range(7)]
    scratch += [
        v(8, 128), v(8, 128), v(8, 8, 128), v(8, 8, 128),
        v(16, 256), v(16, 256), v(32, 16, 256), v(32, 16, 256),
        v(256, 128), v(256, 128), v(8, 128), v(8, 128), v(8, 128), v(8, 128),
        v(8, 8, 128), v(32, 8, 128), v(8, 8, 128), v(32, 8, 128),
    ]
    scratch += [
        pltpu.SemaphoreType.DMA((12,)),
        pltpu.SemaphoreType.DMA((PHASES,)),
        pltpu.SemaphoreType.DMA((PHASES,)),
        pltpu.SemaphoreType.DMA((4, 9)),
        pltpu.SemaphoreType.DMA((4, 9)),
    ]
    coef, rtp_map = pl.pallas_call(
        kernel,
        out_shape=(
            jax.ShapeDtypeStruct((8, 128), F32),
            jax.ShapeDtypeStruct((16, FULL), F32),
        ),
        in_specs=[smem] * 5 + [hbm, vmem, vmem] + [hbm] * len(consts),
        out_specs=(vmem, vmem),
        scratch_shapes=scratch,
        compiler_params=pltpu.CompilerParams(
            collective_id=0, has_side_effects=True, vmem_limit_bytes=60 * 1024 * 1024
        ),
    )(
        foot, where_code, counts.reshape(1), params, jnp.asarray(table["twist_coarse"]),
        kernel_tiles.reshape(9, 256, 512), readings.reshape(1, 256),
        resid_grid.reshape(block), *consts,
    )
    return coef[:4].reshape(1, 1, 512), rtp_map


def solution(mesh):
    in_specs = (
        P("row", "col", None, None, None),
        P("row", "col", None),
        P("row", "col"),
        P("row", "col", None),
        P(),
        P(),
        P(),
        P(),
        P("col", "row"),
    )
    out_specs = (P("row", "col", None), P(("row", "col"), None))
    return jax.shard_map(
        on_device, mesh=mesh, in_specs=in_specs, out_specs=out_specs, check_vma=False
    )
```

time: 771 us -> 103 us (0.13)
  the two profiles are of different devices: /device:TPU:1 before, /device:TPU:46 now
where the time goes in v1:
time: 103 us
  Pallas kernels  95.1 us (92%)
  local copies, waits for them, and re-layouts  4.92 us (5%)
  between operations  1.93 us (2%)
  other arithmetic  1.25 us (1%)
    pallas_call x1, Pallas kernels, on_device(): pl.pallas_call(kernel, out_shape=(jax.ShapeDtypeStruct((8, 128), F32), ja...  95.1 us

profile of v1, /device:TPU:46, one launch (start us, length us, event | category | flops | bytes accessed | tf_op | source)
XLA Modules:
  0.0 103.2 jit_solution(6004343527295101193)
XLA Ops:
  1.9 1.3 %select_reduce_fusion.where_code = s32[9]{0:T(128)} fusion(s32[9]{0:T(128)} %bitcast.11), kind=kLoop, calls=%fused_computation | loop fusion | flops 234 | bytes 72 | tf_op jit(solution)/shard_map/reduce_sum | solution.py:783
  3.2 0.7 fusion
  3.9 1.3 %concatenate.3.params = f32[11]{0:T(128)} concatenate(f32[1]{0:T(128)S(6)} %copy.25, f32[2]{0:T(128)} %param.26, f32[2]{0:T(128)S(1)} %get-tuple-element.10, f32[2]{0:T(128)S(1)} %get-tuple-element.11, f32[2]{0:T(128)S(1)} %get-tuple-element.7, f32[2]{0:T(128)S(1)} %get-tuple-element.6), dimensions={0} | concatenate | bytes 88 | tf_op jit(solution)/shard_map/concatenate | solution.py:784
  5.2 95.1 %shard_map.212 = (f32[8,128]{1,0:T(8,128)}, f32[16,4096]{1,0:T(8,128)}) custom-call(s32[9]{0:T(128)} %bitcast.12, s32[9]{0:T(128)} %select_reduce_fusion.where_code, s32[1]{0:T(128)} %bitcast.6.counts, f32[11]{0:T(128)} %concatenate.3.params, f32[32,16]{1,0:T(8,128)} %constant.37.clone.twist_coarse, f32[9,256,512]{2,1,0:T(8,128)} %bitcast.7, ...), custom_call_target="tpu_custom_call" | custom-call | tf_op jit(solution)/shard_map/pallas_call | solution.py:825
  100.3 1.3 %slice.3 = f32[4,128]{1,0:T(4,128)} slice(f32[8,128]{1,0:T(8,128)} %get-tuple-element.4), slice={[0:4], [0:128]} | slice | bytes 4096 | tf_op jit(solution)/shard_map/slice | solution.py:842
  101.6 1.7 %copy.26 = f32[16,4096]{1,0:T(8,128)} copy(f32[16,4096]{1,0:T(8,128)} %get-tuple-element.15) | data formatting | bytes 524288

commit v2 on v1

v2 whole, which is shorter than its diff:
```python
import functools
import math

import jax
import jax.numpy as jnp
import ml_dtypes
import numpy as np
from jax import lax
from jax.experimental import pallas as pl
from jax.experimental.pallas import tpu as pltpu
from jax.sharding import PartitionSpec as P

F32 = jnp.float32
BF16 = jnp.bfloat16
MESH = pl.DeviceIdType.MESH
ROWS, COLS = 32, 8
FULL = 4096
REFINE = 16
SLOTS = 256
OFFSETS = tuple((a, b) for a in (-1, 0, 1) for b in (-1, 0, 1))
SCALE = 1.0 / 16777216.0

(T1, T2A, T2B, TWIN, T3P, T3Q, ZP, RP, ZQ, RQ, Z1, R1, Z2, R2) = range(14)
PHASES = 14
RETURN0, COLLECT0, RETURN1, COLLECT1 = range(4)


def halves(x):
    high = x.astype(np.float32).astype(ml_dtypes.bfloat16)
    low = (x - high.astype(np.float64)).astype(np.float32).astype(ml_dtypes.bfloat16)
    return np.stack([high, low])


@functools.lru_cache(maxsize=None)
def tables():
    two_pi = 2.0 * math.pi
    a = np.arange(32)
    ka = np.arange(16)
    n = np.arange(128)
    kn = np.arange(128)
    ang_a = two_pi * np.outer(ka, a) / 32
    outer = np.stack([np.cos(ang_a), -np.sin(ang_a)])
    outer[1, 0] = (-1.0) ** a
    eye = np.eye(16)
    outer_fwd = np.kron(outer.reshape(32, 32), eye)
    inv = np.stack([2 * np.cos(ang_a), -2 * np.sin(ang_a)])
    inv[0, 0] = 1.0
    inv[1, 0] = (-1.0) ** a
    pick = eye.reshape(16, 8, 2)
    outer_inv = np.einsum("qphb,tuv->btpuqhv", inv.reshape(2, 8, 2, 32), pick)
    outer_inv = outer_inv.reshape(512, 512)
    ang_t = two_pi * np.outer(ka, n) / 4096
    twist = np.stack([np.cos(ang_t), np.sin(ang_t)])[:, :, None, :]
    twist_tile = np.broadcast_to(
        np.stack([np.cos(ang_t), np.sin(ang_t)]).reshape(2, 8, 1, 1, 2, 1, 128),
        (2, 8, 1, 2, 2, 2, 128),
    ).reshape(2, 8, 1, 8, 128)
    twist_tile = np.concatenate([twist_tile[:1], twist_tile[1:]])
    th = two_pi * np.outer(n, kn) / 128
    c, s = np.cos(th), np.sin(th)
    inner_fwd = np.block([[c, -s], [s, c]])
    inner_inv = np.concatenate([c.T, s.T], axis=1)
    k0 = np.arange(64)
    th0 = two_pi * np.outer(n, 32 * k0) / 4096
    th1 = two_pi * np.outer(n, 16 + 32 * k0) / 4096
    alt = (-1.0) ** n
    first_fwd = np.zeros((256, 256))
    first_fwd[:128, 0:64] = np.cos(th0)
    first_fwd[:128, 128:192] = -np.sin(th0)
    first_fwd[:128, 128] = alt
    first_fwd[128:, 64:128] = np.cos(th1)
    first_fwd[128:, 192:256] = -np.sin(th1)
    first_inv = np.zeros((256, 256))
    first_inv[0:64, :128] = 2 * np.cos(th0).T
    first_inv[0, :128] = 1.0
    first_inv[128:192, :128] = -2 * np.sin(th0).T
    first_inv[128, :128] = alt
    first_inv[64:128, 128:] = 2 * np.cos(th1).T
    first_inv[192:256, 128:] = -2 * np.sin(th1).T
    first_inv = np.concatenate([first_inv[:128], first_inv[128:]], axis=1)
    w = np.arange(512)
    th_w = two_pi * (np.outer(w, w) % 512) / 512
    east = np.concatenate([np.cos(th_w), np.sin(th_w)])
    back = np.array(
        [
            128 * wh + 16 * wm + 2 * t3 + t1
            for t3 in range(8) for wh in range(4) for t1 in range(2) for wm in range(8)
        ]
    )
    east_inv = np.concatenate([np.cos(th_w)[back], np.sin(th_w)[back]])
    kb = np.arange(8)
    ang_c = two_pi * np.outer(np.arange(32), 16 * kb) / 4096
    twist_coarse = np.concatenate([np.cos(ang_c), np.sin(ang_c)], axis=1)
    ang_f = two_pi * np.outer(kb, np.arange(16)) / 4096
    twist_fine = np.broadcast_to(
        np.stack([np.cos(ang_f), np.sin(ang_f)])[..., None], (2, 8, 16, 128)
    )
    starts = back[::16]
    ang_c = two_pi * np.outer(starts, kb) / 4096
    back_coarse = np.concatenate([np.cos(ang_c), np.sin(ang_c)], axis=1)
    ang_f = two_pi * np.outer(kb, back[:16]) / 4096
    back_fine = np.broadcast_to(
        np.stack([np.cos(ang_f), np.sin(ang_f)])[..., None], (2, 8, 16, 128)
    )
    u = np.arange(4096)
    g = np.arange(256)
    hat = np.maximum(0.0, 1.0 - np.abs((u[:, None] + 0.5) / REFINE - 0.5 - g[None, :]))
    spec = np.fft.fft(hat, axis=0)
    east_hat = np.stack(
        [np.concatenate([spec[k::8].real, spec[k::8].imag]) for k in range(8)]
    )
    order = np.array(
        [8 * i + 4 * m2 + g4 for i in range(32) for g4 in range(4) for m2 in range(2)]
    )
    north_hat = np.zeros((32, 144, 256))
    lane = np.arange(64)
    for col in range(8):
        for ka1 in range(2):
            for knh in range(2):
                slot = 2 * col + ka1
                ku = slot + 32 * (64 * knh + lane) if slot else 16 * knh + 32 * lane
                idx = col * 4 + ka1 * 2 + knh
                north_hat[idx, :64] = spec[ku].real[:, order]
                north_hat[idx, 64:128] = spec[ku].imag[:, order]
    north_hat[0, 128] = spec[2048].real[order]
    f32 = np.float32
    return dict(
        outer_fwd=halves(outer_fwd),
        outer_inv=halves(outer_inv),
        inner_fwd=halves(inner_fwd),
        inner_inv=halves(inner_inv),
        first_fwd=halves(first_fwd),
        first_inv=halves(first_inv),
        east=halves(east),
        east_inv=halves(east_inv),
        twist_tile=np.ascontiguousarray(twist_tile).astype(f32),
        back_fine=np.ascontiguousarray(back_fine).astype(f32),
        back_coarse=back_coarse.astype(f32),
        twist=twist.astype(f32),
        twist_fine=np.ascontiguousarray(twist_fine).astype(f32),
        twist_coarse=twist_coarse.astype(f32),
        east_hat=np.ascontiguousarray(halves(east_hat).swapaxes(0, 1)),
        north_hat=np.ascontiguousarray(halves(north_hat).swapaxes(0, 1)),
    )


TABLE_NAMES = (
    "outer_fwd",
    "inner_fwd",
    "first_fwd",
    "twist",
    "twist_fine",
    "east",
    "north_hat",
    "east_hat",
    "inner_inv",
    "first_inv",
    "outer_inv",
    "east_inv",
    "twist_tile",
    "back_fine",
)


def split(x):
    high = x.astype(BF16)
    return high, (x - high.astype(F32)).astype(BF16)


def dot3(lhs, rhs, transposed=False):
    dims = (((1,), (1 if transposed else 0,)), ((), ()))

    def one(x, y):
        return lax.dot_general(x, y, dims, preferred_element_type=F32)

    return one(lhs[0], rhs[0]) + (one(lhs[0], rhs[1]) + one(lhs[1], rhs[0]))


def short_transform(values, sign):
    count = len(values)
    if count == 1:
        return values
    even = short_transform(values[0::2], sign)
    odd = short_transform(values[1::2], sign)
    out = [None] * count
    for k in range(count // 2):
        re, im = odd[k]
        if k == 0:
            pass
        elif 4 * k == count:
            re, im = -sign * im, sign * re
        else:
            co = math.cos(2 * math.pi * k / count)
            si = sign * math.sin(2 * math.pi * k / count)
            re, im = re * co - im * si, re * si + im * co
        ere, eim = even[k]
        out[k] = (ere + re, eim + im)
        out[k + count // 2] = (ere - re, eim - im)
    return out


def pole_of(fn, fe, angles):
    radius = jnp.sqrt(fn * fn + fe * fe)
    safe = jnp.where(radius > 0.0, radius, 1.0)
    nn = jnp.where(radius > 0.0, fn / safe, 0.0)
    ne = jnp.where(radius > 0.0, fe / safe, 0.0)
    re = im = None
    for m in range(2):
        vertical = angles[m]
        horizontal = angles[2 + m]
        along = horizontal * (angles[4 + m] * nn + angles[6 + m] * ne)
        inverse = 1.0 / (vertical * vertical + along * along)
        one_re, one_im = vertical * inverse, -along * inverse
        if re is None:
            re, im = one_re, one_im
        else:
            re, im = re * one_re - im * one_im, re * one_im + im * one_re
    return re, im, radius


def lanes_of(shape):
    return lax.broadcasted_iota(jnp.int32, shape, len(shape) - 1)


def signs_of(shape):
    return jnp.where(lanes_of(shape) < 64, 1.0, -1.0).astype(F32)


def swap(x):
    return pltpu.roll(x, 64, axis=x.ndim - 1)


def kernel(
    foot, counts, damping, depth, inclinations, declinations, twist_coarse, back_coarse,
    tiles_hbm, readings, grid,
    outer_fwd_h, inner_fwd_h, first_fwd_h, twist_h, twist_fine_h, east_h,
    north_hat_h, east_hat_h, inner_inv_h, first_inv_h, outer_inv_h,
    east_inv_h, twist_tile_h, back_fine_h,
    coef_out, map_out,
    tiles, outer_fwd, inner_fwd, first_fwd, twist, twist_fine, east,
    north_hat, east_hat, inner_inv, first_inv, outer_inv,
    east_inv, twist_tile, back_fine,
    in1, send2, in2, send3, in3, twin_send, twin_in, send4, in4, send5, in5,
    spec_main, spec_twin, filt,
    spread0, spread1, ret0, ret1, halo0, halo1, chosen,
    p_own, q_own, zp, zq, xp_send, xq_send, xp, xq,
    y_p, y_q, sum1, sum2, sum1b, sum2b, z1, r1, z2, r2,
    load_sem, send_sem, recv_sem, halo_send, halo_recv,
):
    r = lax.axis_index("row")
    c = lax.axis_index("col")
    kb = r // 4
    low2 = r % 4
    special = (c == 0) & (low2 == 0)

    loads = [
        (tiles_hbm, tiles),
        (outer_fwd_h, outer_fwd),
        (inner_fwd_h, inner_fwd),
        (first_fwd_h, first_fwd),
        (twist_h, twist),
        (twist_fine_h, twist_fine),
        (east_h, east),
        (north_hat_h.at[c * 4 + low2], north_hat),
        (east_hat_h.at[kb], east_hat),
        (inner_inv_h, inner_inv),
        (first_inv_h, first_inv),
        (outer_inv_h, outer_inv),
        (east_inv_h, east_inv),
        (twist_tile_h, twist_tile),
        (back_fine_h, back_fine),
    ]
    copies = [
        pltpu.make_async_copy(src, dst, load_sem.at[i]) for i, (src, dst) in enumerate(loads)
    ]
    for one in copies:
        one.start()

    barrier = pltpu.get_barrier_semaphore()

    def greet(row, col):
        pl.semaphore_signal(barrier, inc=1, device_id=(row, col), device_id_type=MESH)

    def exists(a, b):
        return (r + a >= 0) & (r + a < ROWS) & (c + b >= 0) & (c + b < COLS)

    @pl.loop(1, ROWS)
    def _(i):
        greet((r + i) % ROWS, c)

    @pl.loop(1, COLS)
    def _(i):
        greet(r, (c + i) % COLS)

    expected = jnp.int32(ROWS - 1 + COLS - 1)
    for a in (-1, 1):
        for b in (-1, 1):
            there = exists(a, b)
            expected = expected + there.astype(jnp.int32)

            @pl.when(there)
            def _():
                greet(r + a, c + b)


    def push(src, dst, phase, row, col):
        pltpu.make_async_remote_copy(
            src_ref=src, dst_ref=dst, send_sem=send_sem.at[phase], recv_sem=recv_sem.at[phase],
            device_id=(row, col), device_id_type=MESH,
        ).start()

    def keep(src, dst, phase):
        pltpu.make_async_copy(src, dst, recv_sem.at[phase]).start()

    def arrived(dst, phase):
        pltpu.make_async_copy(dst, dst, recv_sem.at[phase]).wait()

    def left(ref, phase):
        pltpu.make_async_copy(ref, ref, send_sem.at[phase]).wait()

    def rows_exchange(src, dst, phase):
        keep(src.at[r], dst.at[r], phase)

        @pl.loop(1, ROWS)
        def _(i):
            row = (r + i) % ROWS
            push(src.at[row], dst.at[r], phase, row, c)

    def cols_exchange(src, dst, phase):
        keep(src.at[c], dst.at[c], phase)

        @pl.loop(1, COLS)
        def _(i):
            col = (c + i) % COLS
            push(src.at[col], dst.at[c], phase, r, col)

    def rows_share(src, dst, phase):
        keep(src, dst.at[r], phase)

        @pl.loop(1, ROWS)
        def _(i):
            push(src, dst.at[r], phase, (r + i) % ROWS, c)

    def cols_share(src, dst, phase):
        keep(src, dst.at[c], phase)

        @pl.loop(1, COLS)
        def _(i):
            push(src, dst.at[c], phase, r, (c + i) % COLS)

    def halo_copy(src, dst, turn, code, row, col):
        return pltpu.make_async_remote_copy(
            src_ref=src, dst_ref=dst,
            send_sem=halo_send.at[turn, code], recv_sem=halo_recv.at[turn, code],
            device_id=(row, col), device_id_type=MESH,
        )

    def return_start(spread, dst, turn):
        for code, (a, b) in enumerate(OFFSETS):
            if code != 4:

                @pl.when(exists(a, b))
                def _():
                    halo_copy(spread.at[code], dst.at[code], turn, code, r + a, c + b).start()

    def collect_start(own, dst, turn):
        for code, (a, b) in enumerate(OFFSETS):
            if code != 4:

                @pl.when(exists(-a, -b))
                def _():
                    halo_copy(own, dst.at[code], turn, code, r - a, c - b).start()

    def halo_wait(src, dst, turn, collecting):
        for code, (a, b) in enumerate(OFFSETS):
            if code != 4:
                away = -1 if collecting else 1
                source = exists(-away * a, -away * b)

                @pl.when(source)
                def _():
                    halo_copy(src, dst.at[code], turn, code, r, c).wait_recv()

                @pl.when(jnp.logical_not(source))
                def _():
                    dst[code] = jnp.zeros((8, 128), F32)

    def halo_left(src, dst, turn, collecting):
        for code, (a, b) in enumerate(OFFSETS):
            if code != 4:
                away = -1 if collecting else 1

                @pl.when(exists(away * a, away * b))
                def _():
                    halo_copy(src, dst.at[code], turn, code, r, c).wait_send()

    sub8 = lax.broadcasted_iota(jnp.int32, (8, 128), 0)

    def spread_of(y, out):
        @pl.loop(0, 9)
        def _(code):
            k = jnp.int32(0)
            for j in range(9):
                k = jnp.where(foot[j] == code, j, k)
            total = jnp.zeros((8, 128), F32)
            for m in range(4):
                acc = [jnp.zeros((8, 128), F32) for _ in range(4)]
                for t in range(32):
                    part = tiles[k, pl.ds(8 * t, 8), pl.ds(128 * m, 128)]
                    acc[t % 4] = acc[t % 4] + part * y[pl.ds(8 * t, 8), :]
                row = jnp.sum((acc[0] + acc[1]) + (acc[2] + acc[3]), axis=0, keepdims=True)
                total = total + jnp.where(sub8 == m, jnp.broadcast_to(row, (8, 128)), 0.0)
            out[code] = total

    def readings_of(blocks, y):
        @pl.loop(0, 8)
        def _(chunk):
            base = pl.multiple_of(32 * chunk, 32)
            acc = [jnp.zeros((8, 128), F32) for _ in range(4)]
            for k in range(9):
                code = foot[k]
                for m in range(4):
                    row = jnp.broadcast_to(blocks[code, pl.ds(m, 1), :], (8, 128))
                    for t in range(4):
                        part = tiles[k, pl.ds(base + 8 * t, 8), pl.ds(128 * m, 128)]
                        acc[t] = acc[t] + part * row
            for t in range(4):
                slot = lax.broadcasted_iota(jnp.int32, (8, 128), 0) + (base + 8 * t)
                total = jnp.sum(acc[t], axis=1, keepdims=True)
                y[pl.ds(base + 8 * t, 8), :] = jnp.where(
                    slot < counts[0], jnp.broadcast_to(total, (8, 128)), 0.0
                )

    def gather_blocks(own, halo):
        for code in range(9):
            chosen[code] = own[...] if code == 4 else halo[code]

    def own_sum(spread, ret):
        total = spread[4]
        for code in range(9):
            if code != 4:
                total = total + ret[code]
        return total

    def total_of(x):
        return jnp.sum(jnp.sum(x, axis=1, keepdims=True), axis=0, keepdims=True)

    lane8 = lanes_of((8, 128))

    def pack(parts):
        out = jnp.zeros((8, 128), F32)
        for i, part in enumerate(parts):
            out = out + jnp.where(
                (lane8 == i) & (sub8 == 0), jnp.broadcast_to(part, (8, 128)), 0.0
            )
        return out

    def unpack(x, i):
        return total_of(jnp.where((lane8 == i) & (sub8 == 0), x, 0.0))

    state = {}
    sign512 = signs_of((512, 128))
    left16 = lanes_of((16, 128)) < 64

    def met():
        pl.semaphore_wait(barrier, expected)

    def grid_rows():
        rows_exchange(grid, in1, T1)

    def right_side():
        eye = lax.broadcasted_iota(jnp.int32, (SLOTS, SLOTS), 0) == lanes_of((SLOTS, SLOTS))
        column = jnp.sum(
            jnp.where(eye, jnp.broadcast_to(readings[...], (SLOTS, SLOTS)), 0.0),
            axis=1, keepdims=True,
        )
        slot_index = lax.broadcasted_iota(jnp.int32, (SLOTS, 128), 0)
        y_q[...] = jnp.where(
            slot_index < counts[0], jnp.broadcast_to(column, (SLOTS, 128)), 0.0
        )
        copies[0].wait()
        spread_of(y_q, spread0)

    def right_side_return():
        return_start(spread0, ret0, RETURN0)

    def north_forward():
        for i in range(1, 4):
            copies[i].wait()
        copies[4].wait()
        arrived(in1, T1)
        outer = dot3(
            (outer_fwd[0], outer_fwd[1]), split(in1[...].reshape(512, 128))
        ).reshape(2, 16, 16, 128)
        tw_c, tw_s = twist[0], twist[1]
        turned = jnp.concatenate(
            [
                (outer[0] * tw_c + outer[1] * tw_s).reshape(256, 128),
                (outer[1] * tw_c - outer[0] * tw_s).reshape(256, 128),
            ],
            axis=1,
        )
        turned_h, turned_l = split(turned)
        send2[...] = dot3((turned_h, turned_l), (inner_fwd[0], inner_fwd[1])).reshape(8, 32, 256)
        send2[0, 0:16, :] = dot3((turned_h[:16], turned_l[:16]), (first_fwd[0], first_fwd[1]))
        cols_exchange(send2, in2, T2A)

    def first_direction():
        halo_wait(spread0.at[4], ret0, RETURN0, False)
        p_own[...] = own_sum(spread0, ret0)
        collect_start(p_own, halo0, COLLECT0)
        cols_share(p_own, zp, ZP)

    def first_image():
        halo_wait(p_own, halo0, COLLECT0, True)
        gather_blocks(p_own, halo0)
        readings_of(chosen, y_p)
        p_val = p_own[...]
        sum1[...] = pack([total_of(y_p[...] * y_p[...]) * (1.0 / 128.0), total_of(p_val * p_val)])
        cols_share(sum1, z1, Z1)
        spread_of(y_p, spread1)
        return_start(spread1, ret1, RETURN1)

    lane_half = lanes_of((8, 128)) // 32

    def coarse_rows(z, out):
        for half in range(2):
            for g in range(4):
                total = jnp.zeros((8, 128), F32)
                for j in range(4):
                    block = z[4 * half + j]
                    shift = (32 * (j - g)) % 128
                    if shift:
                        block = pltpu.roll(block, shift, axis=1)
                    total = jnp.where(lane_half == j, block, total)
                lanes = pl.ds(128 * half, 128)
                out[pl.ds(2 * g, 2), lanes] = total[0:2]
                out[pl.ds(8 + 2 * g, 2), lanes] = total[2:4]

    def first_coarse():
        arrived(zp, ZP)
        coarse_rows(zp, xp_send)
        rows_share(xp_send, xp, RP)

    def east_first():
        copies[5].wait()
        arrived(in2, T2A)
        pairs = short_transform(
            [(in2[b, :, 0:128], in2[b, :, 128:256]) for b in range(8)], -1.0
        )
        lane32 = lanes_of((32, 128))
        sub32 = lax.broadcasted_iota(jnp.int32, (32, 128), 0)
        apart = (lane32 == 0) & (sub32 < 16) & (c == 0)
        for k in range(8):
            re, im = pairs[k]
            other_re, other_im = pairs[(8 - k) % 8]
            main_re = jnp.where(apart, 0.5 * (re + other_re), re)
            main_im = jnp.where(apart, 0.5 * (im - other_im), im)
            twin_re = 0.5 * (im[:16] + other_im[:16])
            twin_im = 0.5 * (other_re[:16] - re[:16])
            co = twist_coarse[r, k]
            si = twist_coarse[r, 8 + k]
            fine_c, fine_s = twist_fine[0, k], twist_fine[1, k]
            tc = co * fine_c - si * fine_s
            ts = si * fine_c + co * fine_s
            for ka1 in range(2):
                xr, xi = main_re[16 * ka1:16 * ka1 + 16], main_im[16 * ka1:16 * ka1 + 16]
                yr, yi = xr * tc + xi * ts, xi * tc - xr * ts
                send3[4 * k + 2 * ka1] = jnp.where(left16, yr, swap(yi))
                send3[4 * k + 2 * ka1 + 1] = jnp.where(left16, swap(yr), yi)
            yr, yi = twin_re * tc + twin_im * ts, twin_im * tc - twin_re * ts
            twin_send[k] = jnp.where(left16, yr, swap(yi))
        rows_exchange(send3, in3, T2B)

        @pl.when(c == 0)
        def _():
            @pl.loop(0, 8)
            def _(k):
                @pl.when(4 * k == r)
                def _():
                    keep(twin_send.at[k], twin_in.at[r], TWIN)

                @pl.when(4 * k != r)
                def _():
                    push(twin_send.at[k], twin_in.at[r], TWIN, 4 * k, c)

    def share_sums(z, mine, out, phase_in, phase_out):
        arrived(z, phase_in)
        half_sum = z[0]
        for i in range(1, 8):
            half_sum = half_sum + z[i]
        mine[...] = half_sum
        rows_share(mine, out, phase_out)

    def first_applied():
        halo_wait(spread1.at[4], ret1, RETURN1, False)
        q_own[...] = own_sum(spread1, ret1) + damping[0] * p_own[...]
        collect_start(q_own, halo1, COLLECT1)
        cols_share(q_own, zq, ZQ)

    def first_sums():
        share_sums(z1, sum1b, r1, Z1, R1)

    def second_image():
        halo_wait(q_own, halo1, COLLECT1, True)
        gather_blocks(q_own, halo1)
        readings_of(chosen, y_q)

    def second_coarse():
        arrived(zq, ZQ)
        coarse_rows(zq, xq_send)
        rows_share(xq_send, xq, RQ)

    def first_step():
        arrived(r1, R1)
        weight = damping[0]
        full_sum = jnp.sum(r1[...], axis=0)
        g00, rr0 = unpack(full_sum, 0), unpack(full_sum, 1)
        step0 = rr0 / (g00 + weight * rr0)
        p_val = p_own[...]
        resid = p_val - step0 * q_own[...]
        yr1 = y_p[...] - step0 * y_q[...]
        sum2[...] = pack(
            [
                total_of(yr1 * yr1) * (1.0 / 128.0),
                total_of(yr1 * y_p[...]) * (1.0 / 128.0),
                total_of(resid * resid),
                total_of(resid * p_val),
            ]
        )
        cols_share(sum2, z2, Z2)
        state.update(step0=step0, p_val=p_val, resid=resid, g00=g00, rr0=rr0)

    def second_sums():
        share_sums(z2, sum2b, r2, Z2, R2)

    def filter_tables():
        knh = low2 % 2
        ka = 2 * c + low2 // 2
        given = [inclinations[0], inclinations[1], declinations[0], declinations[1]]
        spot = jnp.zeros((8, 128), F32)
        for i, one in enumerate(given):
            spot = jnp.where(lane8 == i, one, spot)
        sines, cosines = jnp.sin(spot), jnp.cos(spot)

        def taken(x, i):
            return jnp.max(jnp.where(lane8 == i, x, -2.0)[0:1], axis=1, keepdims=True)

        angles = [taken(sines, 0), taken(sines, 1), taken(cosines, 0), taken(cosines, 1)]
        angles += [taken(cosines, 2), taken(cosines, 3), taken(sines, 2), taken(sines, 3)]

        @pl.loop(0, 16)
        def _(chunk):
            base = pl.multiple_of(32 * chunk, 32)
            shape = (32, 128)
            lane = lanes_of(shape)
            kv = kb + 8 * (lax.broadcasted_iota(jnp.int32, shape, 0) + base)
            ku = jnp.where(ka > 0, ka + 32 * (64 * knh + lane), 16 * knh + 32 * lane)
            ku = jnp.where(lane < 64, ku, 2048)
            fe = jnp.where(kv < 2048, kv, kv - 4096).astype(F32) * (1.0 / 4096.0)
            fn = jnp.where(ku < 2048, ku, ku - 4096).astype(F32) * (1.0 / 4096.0)
            re_a, im_a, radius = pole_of(fn, fe, angles)
            re_b, im_b, _ = pole_of(
                jnp.where(ku == 2048, 0.5, fn), jnp.where(kv == 2048, 0.5, fe), angles
            )
            kappa = (2.0 * math.pi) * radius
            made = [
                (0.5 * SCALE) * (re_a + re_b),
                (0.5 * SCALE) * (im_a + im_b),
                jnp.exp(-kappa * depth[0]),
                jnp.exp(-kappa * depth[1]),
            ]
            for i, one in enumerate(made):
                other = swap(one)
                main = jnp.where(lane < 64, one, other)
                twin = jnp.where(lane < 64, other, one)
                if i == 1:
                    sign = signs_of(shape)
                    main, twin = main * sign, twin * sign
                filt[i, pl.ds(base, 32), :] = main
                filt[4 + i, pl.ds(base, 32), :] = twin

    def east_second():
        copies[6].wait()
        arrived(in3, T2B)

        @pl.when(special)
        def _():
            arrived(twin_in, TWIN)

        @pl.when(jnp.logical_not(special))
        def _():
            twin_in[...] = jnp.zeros((32, 16, 128), F32)

        both = jnp.concatenate(
            [in3[...].reshape(512, 128), twin_in[...].reshape(512, 128)], axis=1
        )
        spun = dot3((east[0], east[1]), split(both))
        spec_main[...] = spun[:512, :128] + sign512 * swap(spun[512:, :128])
        spec_twin[...] = spun[:512, 128:] + sign512 * swap(spun[512:, 128:])

    def second_step():
        arrived(xp, RP)
        arrived(xq, RQ)
        arrived(r2, R2)
        step0, p_val, resid = state["step0"], state["p_val"], state["resid"]
        g00, rr0 = state["g00"], state["rr0"]
        full_sum = jnp.sum(r2[...], axis=0)
        g11, g10 = unpack(full_sum, 0), unpack(full_sum, 1)
        rr1, r10 = unpack(full_sum, 2), unpack(full_sum, 3)
        beta = rr1 / rr0
        bent = (g11 + 2.0 * beta * g10 + beta * beta * g00) + damping[0] * (
            rr1 + 2.0 * beta * r10 + beta * beta * rr0
        )
        step1 = rr1 / bent
        coefs = step0 * p_val + step1 * (resid + beta * p_val)
        for m in range(4):
            coef_out[0, :, pl.ds(128 * m, 128)] = coefs[m:m + 1]
        state.update(alpha=step0 + step1 + step1 * beta, gamma=-step1 * step0)

    def shape_spectrum():
        copies[7].wait()
        copies[8].wait()
        copies[12].wait()
        copies[14].wait()
        alpha, gamma = state["alpha"], state["gamma"]
        rows_of = []
        extra = []
        for layer in range(2):
            coarse = alpha * xp[:, 8 * layer:8 * layer + 8, :].reshape(256, 256) + gamma * xq[
                :, 8 * layer:8 * layer + 8, :
            ].reshape(256, 256)
            north = dot3((north_hat[0], north_hat[1]), split(coarse))
            rows_of.append(north[:128])
            extra.append(north[128:144])
        rows_of.extend(extra)
        rows_of.append(jnp.zeros((96, 256), F32))
        model = dot3(
            (east_hat[0], east_hat[1]), split(jnp.concatenate(rows_of, axis=0)), transposed=True
        )
        left512 = lanes_of((512, 128)) < 64
        total = spec_main[...]
        twin = spec_twin[...]
        for layer in range(2):
            lanes = slice(128 * layer, 128 * layer + 128)
            plane = model[:512, lanes] - sign512 * swap(model[512:, lanes])
            total = total + filt[2 + layer] * plane
            top, bottom = model[:512, 256:], model[512:, 256:]
            if layer:
                top = pltpu.roll(top, 112, axis=1)
                bottom = pltpu.roll(bottom, 112, axis=1)
            twin = twin + filt[6 + layer] * jnp.where(left512, top, swap(bottom))
        shaped = filt[0] * total - filt[1] * swap(total)
        shaped_twin = filt[4] * twin - filt[5] * swap(twin)
        joined = special & (lanes_of((512, 128)) % 64 == 0)
        state["shaped"] = shaped - jnp.where(joined, sign512 * swap(shaped_twin), 0.0)

    def east_back():
        spun = dot3((east_inv[0], east_inv[1]), split(state["shaped"]))
        back = spun[:512] - sign512 * swap(spun[512:])
        sign16 = signs_of((16, 128))
        fine_c, fine_s = back_fine[0, kb], back_fine[1, kb]
        for chunk in range(32):
            block = back[16 * chunk:16 * chunk + 16]
            co = back_coarse[chunk, kb]
            si = back_coarse[chunk, 8 + kb]
            tc = co * fine_c - si * fine_s
            ts = si * fine_c + co * fine_s
            send4[chunk] = block * tc - sign16 * ts * swap(block)
        rows_exchange(send4, in4, T3P)

    def east_last():
        arrived(in4, T3P)
        for ka1 in range(2):
            values = []
            for k in range(8):
                m0, m1 = in4[4 * k + 2 * ka1], in4[4 * k + 2 * ka1 + 1]
                values.append((jnp.where(left16, m0, swap(m1)), jnp.where(left16, swap(m0), m1)))
            for b, (re, im) in enumerate(short_transform(values, 1.0)):
                for t1 in range(2):
                    rows = slice(8 * t1, 8 * t1 + 8)
                    send5[b, pl.ds(2 * ka1 + t1, 8, stride=8), :] = re[rows]
                    send5[b, pl.ds(4 + 2 * ka1 + t1, 8, stride=8), :] = im[rows]

        def tile(b, wm):
            return send5.at[b, pl.ds(pl.multiple_of(8 * wm, 8), 8)]

        keep(tile(kb, c), in5.at[c, kb], T3Q)

        @pl.loop(1, 64)
        def _(i):
            b = (kb + i // 8) % COLS
            wm = (c + i) % COLS
            push(tile(b, wm), in5.at[c, kb], T3Q, 4 * b + low2, wm)

    def north_back():
        for i in range(9, 12):
            copies[i].wait()
        copies[13].wait()
        arrived(in5, T3Q)
        halves_in = split(in5[...].reshape(512, 128))
        inner = dot3(halves_in, (inner_inv[0], inner_inv[1]))
        first = dot3((halves_in[0][:64], halves_in[1][:64]), (first_inv[0], first_inv[1]))
        shape = (64, 8, 128)
        row = lax.broadcasted_iota(jnp.int32, shape, 1)
        sign = jnp.where(row < 4, -1.0, 1.0)

        def cross(x):
            return pltpu.roll(x, 4, axis=1)

        both = inner[:, :128].reshape(shape) + sign * cross(inner[:, 128:].reshape(shape))
        rr, ri, ir, ii = [first[:, 128 * i:128 * i + 128].reshape(8, 8, 128) for i in range(4)]
        low = row[:8] < 4
        joint = jnp.where(low, rr + cross(ir), ii + cross(ri))
        both = jnp.concatenate([jnp.where(row[:8] % 4 < 2, joint, both[:8]), both[8:]], axis=0)
        shape = (8, 8, 8, 128)
        turned = both.reshape(shape) * twist_tile[0] + (sign * cross(both)).reshape(
            shape
        ) * twist_tile[1]
        final = dot3((outer_inv[0], outer_inv[1]), split(turned.reshape(512, 128)))
        for i in range(32):
            map_out[:, pl.ds(128 * i, 128)] = final[16 * i:16 * i + 16]

    filter_tables()
    right_side()
    met()
    grid_rows()
    right_side_return()
    north_forward()
    first_direction()
    first_image()
    first_coarse()
    east_first()
    first_applied()
    first_sums()
    second_image()
    second_coarse()
    first_step()
    east_second()
    second_sums()
    second_step()
    shape_spectrum()
    east_back()
    east_last()
    north_back()

    for buf, phase in ((in1, T1), (send3, T2B), (send4, T3P), (xp, RP), (xq, RQ), (r1, R1), (r2, R2)):
        left(buf.at[pl.ds(0, ROWS - 1)], phase)
    for buf, phase in ((send2, T2A), (zp, ZP), (zq, ZQ), (z1, Z1), (z2, Z2)):
        left(buf.at[pl.ds(0, COLS - 1)], phase)

    left(send5.at[pl.ds(0, 7)], T3Q)
    left(send5.at[0, pl.ds(0, 56)], T3Q)

    @pl.when((c == 0) & (low2 == 0))
    def _():
        left(twin_send.at[pl.ds(0, 7)], TWIN)

    @pl.when((c == 0) & (low2 != 0))
    def _():
        left(twin_send, TWIN)

    halo_left(spread0.at[4], ret0, RETURN0, False)
    halo_left(p_own, halo0, COLLECT0, True)
    halo_left(spread1.at[4], ret1, RETURN1, False)
    halo_left(q_own, halo1, COLLECT1, True)


def on_device(
    kernel_tiles, footprints, counts, readings, damping, layer_depth,
    inclinations, declinations, resid_grid,
):
    table = tables()
    consts = [jnp.asarray(table[name]) for name in TABLE_NAMES]
    shapes = [x.shape for x in consts]
    shapes[6] = shapes[6][1:]
    shapes[7] = shapes[7][1:]
    kinds = [x.dtype for x in consts]
    smem = pl.BlockSpec(memory_space=pltpu.SMEM)
    vmem = pl.BlockSpec(memory_space=pltpu.VMEM)
    hbm = pl.BlockSpec(memory_space=pl.ANY)

    def v(*shape):
        return pltpu.VMEM(shape, F32)

    block = (32, 16, 128)
    scratch = [v(9, 256, 512)]
    scratch += [pltpu.VMEM(shape, kind) for shape, kind in zip(shapes, kinds)]
    scratch += [
        v(*block), v(8, 32, 256), v(8, 32, 256), v(*block), v(*block),
        v(8, 16, 128), v(*block), v(*block), v(*block), v(8, 64, 128), v(8, 8, 8, 128),
        v(512, 128), v(512, 128), v(8, 512, 128),
    ]
    scratch += [v(9, 8, 128) for _ in range(7)]
    scratch += [
        v(8, 128), v(8, 128), v(8, 8, 128), v(8, 8, 128),
        v(16, 256), v(16, 256), v(32, 16, 256), v(32, 16, 256),
        v(256, 128), v(256, 128), v(8, 128), v(8, 128), v(8, 128), v(8, 128),
        v(8, 8, 128), v(32, 8, 128), v(8, 8, 128), v(32, 8, 128),
    ]
    scratch += [
        pltpu.SemaphoreType.DMA((15,)),
        pltpu.SemaphoreType.DMA((PHASES,)),
        pltpu.SemaphoreType.DMA((PHASES,)),
        pltpu.SemaphoreType.DMA((4, 9)),
        pltpu.SemaphoreType.DMA((4, 9)),
    ]
    coef, rtp_map = pl.pallas_call(
        kernel,
        out_shape=(
            jax.ShapeDtypeStruct((1, 1, 512), F32),
            jax.ShapeDtypeStruct((16, FULL), F32),
        ),
        in_specs=[smem] * 8 + [hbm, vmem, vmem] + [hbm] * len(consts),
        out_specs=(vmem, vmem),
        scratch_shapes=scratch,
        compiler_params=pltpu.CompilerParams(
            collective_id=0, has_side_effects=True, vmem_limit_bytes=60 * 1024 * 1024
        ),
    )(
        footprints.reshape(9), counts.reshape(1), damping, layer_depth,
        inclinations, declinations,
        jnp.asarray(table["twist_coarse"]), jnp.asarray(table["back_coarse"]),
        kernel_tiles.reshape(9, 256, 512), readings.reshape(1, 256),
        resid_grid.reshape(block), *consts,
    )
    return coef, rtp_map


def solution(mesh):
    in_specs = (
        P("row", "col", None, None, None),
        P("row", "col", None),
        P("row", "col"),
        P("row", "col", None),
        P(),
        P(),
        P(),
        P(),
        P("col", "row"),
    )
    out_specs = (P("row", "col", None), P(("row", "col"), None))
    return jax.shard_map(
        on_device, mesh=mesh, in_specs=in_specs, out_specs=out_specs, check_vma=False
    )
```

time: 103 us -> 85.1 us (0.83)
  the two profiles are of different devices: /device:TPU:46 before, /device:TPU:1 now
where the time goes in v2:
time: 85.1 us; the launch traced here: 84.9 us
  Pallas kernels  80.1 us (94%)
  local copies, waits for them, and re-layouts  2.92 us (3%)
  between operations  1.93 us (2%)
    pallas_call x1, Pallas kernels, on_device(): pl.pallas_call(kernel, out_shape=(jax.ShapeDtypeStruct((1, 1, 512), F32),...  80.1 us
    unnamed x2, local copies, waits for them, and re-layouts  2.92 us

profile of v2, /device:TPU:1, one launch (start us, length us, event | category | flops | bytes accessed | tf_op | source)
XLA Modules:
  0.0 84.9 jit_solution(8195915910798170798)
XLA Ops:
  1.9 80.1 %shard_map.248 = (f32[1,1,512]{2,1,0:T(1,128)}, f32[16,4096]{1,0:T(8,128)}) custom-call(s32[9]{0:T(128)} %bitcast.9, s32[1]{0:T(128)} %bitcast.5.counts, f32[1]{0:T(128)S(6)} %copy.30.damping, f32[2]{0:T(128)} %depth.1, f32[2]{0:T(128)} %inclinations.1, f32[2]{0:T(128)} %declinations.1, f32[32,16]{1,0:T(8,128)} %constant.46.clone.twist_coarse, ...), custom_call_target="tpu_custom_call" | custom-call | tf_op jit(solution)/shard_map/pallas_call | solution.py:908
  82.0 1.2 %copy.31 = f32[1,1,512]{2,1,0:T(1,128)} copy(f32[1,1,512]{2,1,0:T(1,128)} %get-tuple-element.4) | data formatting | bytes 4096
  83.2 1.7 %copy.32 = f32[16,4096]{1,0:T(8,128)} copy(f32[16,4096]{1,0:T(8,128)} %get-tuple-element.5) | data formatting | bytes 524288

commit v3 on v2

--- a/solution.py
+++ b/solution.py
@@ -20,8 +20,8 @@
 OFFSETS = tuple((a, b) for a in (-1, 0, 1) for b in (-1, 0, 1))
 SCALE = 1.0 / 16777216.0
 
-(T1, T2A, T2B, TWIN, T3P, T3Q, ZP, RP, ZQ, RQ, Z1, R1, Z2, R2) = range(14)
-PHASES = 14
+(T1, T2A, T2B, TWIN, T3P, T3Q, ZP, RP, ZQ, RQ, Z1, R1, Z2, R2, RP2, RQ2) = range(16)
+PHASES = 16
 RETURN0, COLLECT0, RETURN1, COLLECT1 = range(4)
 
 
@@ -46,20 +46,13 @@
     inv = np.stack([2 * np.cos(ang_a), -2 * np.sin(ang_a)])
     inv[0, 0] = 1.0
     inv[1, 0] = (-1.0) ** a
-    pick = eye.reshape(16, 8, 2)
-    outer_inv = np.einsum("qphb,tuv->btpuqhv", inv.reshape(2, 8, 2, 32), pick)
-    outer_inv = outer_inv.reshape(512, 512)
+    outer_inv = np.kron(inv.reshape(32, 32).T, eye)
     ang_t = two_pi * np.outer(ka, n) / 4096
     twist = np.stack([np.cos(ang_t), np.sin(ang_t)])[:, :, None, :]
-    twist_tile = np.broadcast_to(
-        np.stack([np.cos(ang_t), np.sin(ang_t)]).reshape(2, 8, 1, 1, 2, 1, 128),
-        (2, 8, 1, 2, 2, 2, 128),
-    ).reshape(2, 8, 1, 8, 128)
-    twist_tile = np.concatenate([twist_tile[:1], twist_tile[1:]])
     th = two_pi * np.outer(n, kn) / 128
     c, s = np.cos(th), np.sin(th)
     inner_fwd = np.block([[c, -s], [s, c]])
-    inner_inv = np.concatenate([c.T, s.T], axis=1)
+    inner_inv = np.block([[c.T, s.T], [-s.T, c.T]])
     k0 = np.arange(64)
     th0 = two_pi * np.outer(n, 32 * k0) / 4096
     th1 = two_pi * np.outer(n, 16 + 32 * k0) / 4096
@@ -77,29 +70,20 @@
     first_inv[128, :128] = alt
     first_inv[64:128, 128:] = 2 * np.cos(th1).T
     first_inv[192:256, 128:] = -2 * np.sin(th1).T
-    first_inv = np.concatenate([first_inv[:128], first_inv[128:]], axis=1)
+    by_half = np.concatenate(
+        [np.arange(64), 128 + np.arange(64), 64 + np.arange(64), 192 + np.arange(64)]
+    )
+    inner_inv, first_inv = inner_inv[by_half], first_inv[by_half]
     w = np.arange(512)
     th_w = two_pi * (np.outer(w, w) % 512) / 512
     east = np.concatenate([np.cos(th_w), np.sin(th_w)])
-    back = np.array(
-        [
-            128 * wh + 16 * wm + 2 * t3 + t1
-            for t3 in range(8) for wh in range(4) for t1 in range(2) for wm in range(8)
-        ]
-    )
+    back = np.arange(512).reshape(4, 8, 16).transpose(1, 0, 2).reshape(512)
     east_inv = np.concatenate([np.cos(th_w)[back], np.sin(th_w)[back]])
     kb = np.arange(8)
     ang_c = two_pi * np.outer(np.arange(32), 16 * kb) / 4096
     twist_coarse = np.concatenate([np.cos(ang_c), np.sin(ang_c)], axis=1)
     ang_f = two_pi * np.outer(kb, np.arange(16)) / 4096
     twist_fine = np.broadcast_to(
-        np.stack([np.cos(ang_f), np.sin(ang_f)])[..., None], (2, 8, 16, 128)
-    )
-    starts = back[::16]
-    ang_c = two_pi * np.outer(starts, kb) / 4096
-    back_coarse = np.concatenate([np.cos(ang_c), np.sin(ang_c)], axis=1)
-    ang_f = two_pi * np.outer(kb, back[:16]) / 4096
-    back_fine = np.broadcast_to(
         np.stack([np.cos(ang_f), np.sin(ang_f)])[..., None], (2, 8, 16, 128)
     )
     u = np.arange(4096)
@@ -110,7 +94,10 @@
         [np.concatenate([spec[k::8].real, spec[k::8].imag]) for k in range(8)]
     )
     order = np.array(
-        [8 * i + 4 * m2 + g4 for i in range(32) for g4 in range(4) for m2 in range(2)]
+        [
+            8 * (2 * chip + core) + 4 * m2 + g4
+            for core in range(2) for chip in range(16) for g4 in range(4) for m2 in range(2)
+        ]
     )
     north_hat = np.zeros((32, 144, 256))
     lane = np.arange(64)
@@ -133,9 +120,6 @@
         first_inv=halves(first_inv),
         east=halves(east),
         east_inv=halves(east_inv),
-        twist_tile=np.ascontiguousarray(twist_tile).astype(f32),
-        back_fine=np.ascontiguousarray(back_fine).astype(f32),
-        back_coarse=back_coarse.astype(f32),
         twist=twist.astype(f32),
         twist_fine=np.ascontiguousarray(twist_fine).astype(f32),
         twist_coarse=twist_coarse.astype(f32),
@@ -157,8 +141,6 @@
     "first_inv",
     "outer_inv",
     "east_inv",
-    "twist_tile",
-    "back_fine",
 )
 
 
@@ -231,15 +213,15 @@
 
 
 def kernel(
-    foot, counts, damping, depth, inclinations, declinations, twist_coarse, back_coarse,
+    foot, counts, damping, depth, inclinations, declinations, twist_coarse,
     tiles_hbm, readings, grid,
     outer_fwd_h, inner_fwd_h, first_fwd_h, twist_h, twist_fine_h, east_h,
     north_hat_h, east_hat_h, inner_inv_h, first_inv_h, outer_inv_h,
-    east_inv_h, twist_tile_h, back_fine_h,
+    east_inv_h,
     coef_out, map_out,
     tiles, outer_fwd, inner_fwd, first_fwd, twist, twist_fine, east,
     north_hat, east_hat, inner_inv, first_inv, outer_inv,
-    east_inv, twist_tile, back_fine,
+    east_inv,
     in1, send2, in2, send3, in3, twin_send, twin_in, send4, in4, send5, in5,
     spec_main, spec_twin, filt,
     spread0, spread1, ret0, ret1, halo0, halo1, chosen,
@@ -249,9 +231,9 @@
 ):
     r = lax.axis_index("row")
     c = lax.axis_index("col")
-    kb = r // 4
+    group = r // 4
     low2 = r % 4
-    special = (c == 0) & (low2 == 0)
+    special = r == 0
 
     loads = [
         (tiles_hbm, tiles),
@@ -261,20 +243,17 @@
         (twist_h, twist),
         (twist_fine_h, twist_fine),
         (east_h, east),
-        (north_hat_h.at[c * 4 + low2], north_hat),
-        (east_hat_h.at[kb], east_hat),
+        (north_hat_h.at[r], north_hat),
+        (east_hat_h.at[c], east_hat),
         (inner_inv_h, inner_inv),
         (first_inv_h, first_inv),
         (outer_inv_h, outer_inv),
         (east_inv_h, east_inv),
-        (twist_tile_h, twist_tile),
-        (back_fine_h, back_fine),
     ]
     copies = [
         pltpu.make_async_copy(src, dst, load_sem.at[i]) for i, (src, dst) in enumerate(loads)
     ]
-    for one in copies:
-        one.start()
+    copies[0].start()
 
     barrier = pltpu.get_barrier_semaphore()
 
@@ -318,35 +297,61 @@
     def left(ref, phase):
         pltpu.make_async_copy(ref, ref, send_sem.at[phase]).wait()
 
+    def far_col(j):
+        half = (j + 1) // 2
+        return (c + jnp.where(j % 2 == 1, 4 - half, 4 + half)) % COLS
+
+    def far_row(j):
+        def step(i):
+            return jnp.where(i == 0, 2, jnp.where(i == 3, 0, 2 * i - 1))
+
+        x = (r // 8 + step(j // 8)) % 4
+        y = (r // 2 + step(j // 2 % 4)) % 4
+        return 8 * x + 2 * y + (r + 1 + j) % 2
+
     def rows_exchange(src, dst, phase):
         keep(src.at[r], dst.at[r], phase)
 
-        @pl.loop(1, ROWS)
+        @pl.loop(0, ROWS - 1)
         def _(i):
-            row = (r + i) % ROWS
+            row = far_row(i)
             push(src.at[row], dst.at[r], phase, row, c)
 
     def cols_exchange(src, dst, phase):
         keep(src.at[c], dst.at[c], phase)
 
-        @pl.loop(1, COLS)
+        @pl.loop(0, COLS - 1)
         def _(i):
-            col = (c + i) % COLS
+            col = far_col(i)
             push(src.at[col], dst.at[c], phase, r, col)
 
     def rows_share(src, dst, phase):
         keep(src, dst.at[r], phase)
 
-        @pl.loop(1, ROWS)
+        @pl.loop(0, ROWS - 1)
         def _(i):
-            push(src, dst.at[r], phase, (r + i) % ROWS, c)
+            push(src, dst.at[r], phase, far_row(i), c)
+
+    core = r % 2
+    chip = r // 2
+
+    def chips_share(src, dst, phase):
+        keep(src, dst.at[core, chip], phase)
+
+        @pl.loop(0, ROWS // 2 - 1)
+        def _(i):
+            push(src, dst.at[core, chip], phase, far_row(2 * i + 1), c)
+
+    def chip_share(dst, phase_in, phase_out):
+        arrived(dst.at[core], phase_in)
+        push(dst.at[core], dst.at[core], phase_out, r + 1 - 2 * core, c)
 
     def cols_share(src, dst, phase):
         keep(src, dst.at[c], phase)
 
-        @pl.loop(1, COLS)
+        @pl.loop(0, COLS - 1)
         def _(i):
-            push(src, dst.at[c], phase, r, (c + i) % COLS)
+            push(src, dst.at[c], phase, r, far_col(i))
 
     def halo_copy(src, dst, turn, code, row, col):
         return pltpu.make_async_remote_copy(
@@ -479,6 +484,8 @@
             slot_index < counts[0], jnp.broadcast_to(column, (SLOTS, 128)), 0.0
         )
         copies[0].wait()
+        for one in copies[1:]:
+            one.start()
         spread_of(y_q, spread0)
 
     def right_side_return():
@@ -540,7 +547,7 @@
     def first_coarse():
         arrived(zp, ZP)
         coarse_rows(zp, xp_send)
-        rows_share(xp_send, xp, RP)
+        chips_share(xp_send, xp, RP)
 
     def east_first():
         copies[5].wait()
@@ -570,19 +577,33 @@
                 send3[4 * k + 2 * ka1 + 1] = jnp.where(left16, swap(yr), yi)
             yr, yi = twin_re * tc + twin_im * ts, twin_im * tc - twin_re * ts
             twin_send[k] = jnp.where(left16, yr, swap(yi))
-        rows_exchange(send3, in3, T2B)
+        mine = group == c
+
+        @pl.loop(0, ROWS)
+        def _(i):
+            k = far_col(i // 4)
+            low = (low2 + i) % 4
+            block = send3.at[4 * k + low]
+
+            @pl.when(mine & (k == c) & (low == low2))
+            def _():
+                keep(block, in3.at[r], T2B)
+
+            @pl.when(jnp.logical_not(mine & (k == c) & (low == low2)))
+            def _():
+                push(block, in3.at[r], T2B, 4 * c + low, k)
 
         @pl.when(c == 0)
         def _():
-            @pl.loop(0, 8)
+            @pl.loop(0, COLS)
             def _(k):
-                @pl.when(4 * k == r)
+                @pl.when((k == 0) & (r == 0))
                 def _():
                     keep(twin_send.at[k], twin_in.at[r], TWIN)
 
-                @pl.when(4 * k != r)
+                @pl.when(jnp.logical_not((k == 0) & (r == 0)))
                 def _():
-                    push(twin_send.at[k], twin_in.at[r], TWIN, 4 * k, c)
+                    push(twin_send.at[k], twin_in.at[r], TWIN, 0, k)
 
     def share_sums(z, mine, out, phase_in, phase_out):
         arrived(z, phase_in)
@@ -598,6 +619,12 @@
         collect_start(q_own, halo1, COLLECT1)
         cols_share(q_own, zq, ZQ)
 
+    def first_spread():
+        chip_share(xp, RP, RP2)
+
+    def second_spread():
+        chip_share(xq, RQ, RQ2)
+
     def first_sums():
         share_sums(z1, sum1b, r1, Z1, R1)
 
@@ -609,7 +636,7 @@
     def second_coarse():
         arrived(zq, ZQ)
         coarse_rows(zq, xq_send)
-        rows_share(xq_send, xq, RQ)
+        chips_share(xq_send, xq, RQ)
 
     def first_step():
         arrived(r1, R1)
@@ -636,7 +663,7 @@
 
     def filter_tables():
         knh = low2 % 2
-        ka = 2 * c + low2 // 2
+        ka = 2 * group + low2 // 2
         given = [inclinations[0], inclinations[1], declinations[0], declinations[1]]
         spot = jnp.zeros((8, 128), F32)
         for i, one in enumerate(given):
@@ -654,7 +681,7 @@
             base = pl.multiple_of(32 * chunk, 32)
             shape = (32, 128)
             lane = lanes_of(shape)
-            kv = kb + 8 * (lax.broadcasted_iota(jnp.int32, shape, 0) + base)
+            kv = c + 8 * (lax.broadcasted_iota(jnp.int32, shape, 0) + base)
             ku = jnp.where(ka > 0, ka + 32 * (64 * knh + lane), 16 * knh + 32 * lane)
             ku = jnp.where(lane < 64, ku, 2048)
             fe = jnp.where(kv < 2048, kv, kv - 4096).astype(F32) * (1.0 / 4096.0)
@@ -700,8 +727,8 @@
         spec_twin[...] = spun[:512, 128:] + sign512 * swap(spun[512:, 128:])
 
     def second_step():
-        arrived(xp, RP)
-        arrived(xq, RQ)
+        arrived(xp.at[1 - core], RP2)
+        arrived(xq.at[1 - core], RQ2)
         arrived(r2, R2)
         step0, p_val, resid = state["step0"], state["p_val"], state["resid"]
         g00, rr0 = state["g00"], state["rr0"]
@@ -722,14 +749,13 @@
         copies[7].wait()
         copies[8].wait()
         copies[12].wait()
-        copies[14].wait()
         alpha, gamma = state["alpha"], state["gamma"]
         rows_of = []
         extra = []
         for layer in range(2):
-            coarse = alpha * xp[:, 8 * layer:8 * layer + 8, :].reshape(256, 256) + gamma * xq[
-                :, 8 * layer:8 * layer + 8, :
-            ].reshape(256, 256)
+            coarse = alpha * xp[:, :, 8 * layer:8 * layer + 8, :].reshape(
+                256, 256
+            ) + gamma * xq[:, :, 8 * layer:8 * layer + 8, :].reshape(256, 256)
             north = dot3((north_hat[0], north_hat[1]), split(coarse))
             rows_of.append(north[:128])
             extra.append(north[128:144])
@@ -759,104 +785,103 @@
         spun = dot3((east_inv[0], east_inv[1]), split(state["shaped"]))
         back = spun[:512] - sign512 * swap(spun[512:])
         sign16 = signs_of((16, 128))
-        fine_c, fine_s = back_fine[0, kb], back_fine[1, kb]
-        for chunk in range(32):
-            block = back[16 * chunk:16 * chunk + 16]
-            co = back_coarse[chunk, kb]
-            si = back_coarse[chunk, 8 + kb]
-            tc = co * fine_c - si * fine_s
-            ts = si * fine_c + co * fine_s
-            send4[chunk] = block * tc - sign16 * ts * swap(block)
-        rows_exchange(send4, in4, T3P)
+        fine_c, fine_s = twist_fine[0, c], twist_fine[1, c]
+        for mid in range(8):
+            for top in range(4):
+                base = 64 * mid + 16 * top
+                block = back[base:base + 16]
+                co = twist_coarse[8 * top + mid, c]
+                si = twist_coarse[8 * top + mid, 8 + c]
+                tc = co * fine_c - si * fine_s
+                ts = si * fine_c + co * fine_s
+                send4[mid, 16 * top:16 * top + 16, :] = block * tc - sign16 * ts * swap(block)
+        cols_exchange(send4, in4, T3P)
 
     def east_last():
         arrived(in4, T3P)
-        for ka1 in range(2):
+        for pair in range(2):
             values = []
             for k in range(8):
-                m0, m1 = in4[4 * k + 2 * ka1], in4[4 * k + 2 * ka1 + 1]
+                m0 = in4[k, 32 * pair:32 * pair + 16, :]
+                m1 = in4[k, 32 * pair + 16:32 * pair + 32, :]
                 values.append((jnp.where(left16, m0, swap(m1)), jnp.where(left16, swap(m0), m1)))
             for b, (re, im) in enumerate(short_transform(values, 1.0)):
-                for t1 in range(2):
-                    rows = slice(8 * t1, 8 * t1 + 8)
-                    send5[b, pl.ds(2 * ka1 + t1, 8, stride=8), :] = re[rows]
-                    send5[b, pl.ds(4 + 2 * ka1 + t1, 8, stride=8), :] = im[rows]
-
-        def tile(b, wm):
-            return send5.at[b, pl.ds(pl.multiple_of(8 * wm, 8), 8)]
-
-        keep(tile(kb, c), in5.at[c, kb], T3Q)
-
-        @pl.loop(1, 64)
-        def _(i):
-            b = (kb + i // 8) % COLS
-            wm = (c + i) % COLS
-            push(tile(b, wm), in5.at[c, kb], T3Q, 4 * b + low2, wm)
+                send5[4 * b + 2 * pair] = jnp.where(left16, re, swap(im))
+                send5[4 * b + 2 * pair + 1] = jnp.where(left16, swap(re), im)
+        rows_exchange(send5, in5, T3Q)
 
     def north_back():
         for i in range(9, 12):
             copies[i].wait()
-        copies[13].wait()
         arrived(in5, T3Q)
-        halves_in = split(in5[...].reshape(512, 128))
-        inner = dot3(halves_in, (inner_inv[0], inner_inv[1]))
-        first = dot3((halves_in[0][:64], halves_in[1][:64]), (first_inv[0], first_inv[1]))
-        shape = (64, 8, 128)
-        row = lax.broadcasted_iota(jnp.int32, shape, 1)
-        sign = jnp.where(row < 4, -1.0, 1.0)
-
-        def cross(x):
-            return pltpu.roll(x, 4, axis=1)
-
-        both = inner[:, :128].reshape(shape) + sign * cross(inner[:, 128:].reshape(shape))
-        rr, ri, ir, ii = [first[:, 128 * i:128 * i + 128].reshape(8, 8, 128) for i in range(4)]
-        low = row[:8] < 4
-        joint = jnp.where(low, rr + cross(ir), ii + cross(ri))
-        both = jnp.concatenate([jnp.where(row[:8] % 4 < 2, joint, both[:8]), both[8:]], axis=0)
-        shape = (8, 8, 8, 128)
-        turned = both.reshape(shape) * twist_tile[0] + (sign * cross(both)).reshape(
-            shape
-        ) * twist_tile[1]
-        final = dot3((outer_inv[0], outer_inv[1]), split(turned.reshape(512, 128)))
+        tw_c, tw_s = twist[0], twist[1]
+        come = in5[...].reshape(16, 2, 16, 128)
+        pair = jnp.concatenate(
+            [come[:, 0].reshape(256, 128), come[:, 1].reshape(256, 128)], axis=1
+        )
+        pair_h, pair_l = split(pair)
+        inner = dot3((pair_h, pair_l), (inner_inv[0], inner_inv[1]))
+        first = dot3((pair_h[:16], pair_l[:16]), (first_inv[0], first_inv[1]))
+        inner = jnp.concatenate([first, inner[16:]], axis=0)
+        re, im = inner[:, :128].reshape(16, 16, 128), inner[:, 128:].reshape(16, 16, 128)
+        turned = jnp.concatenate(
+            [
+                (re * tw_c - im * tw_s).reshape(256, 128),
+                (im * tw_c + re * tw_s).reshape(256, 128),
+            ],
+            axis=0,
+        )
+        final = dot3((outer_inv[0], outer_inv[1]), split(turned))
         for i in range(32):
             map_out[:, pl.ds(128 * i, 128)] = final[16 * i:16 * i + 16]
 
-    filter_tables()
     right_side()
     met()
+    right_side_return()
     grid_rows()
-    right_side_return()
-    north_forward()
+    filter_tables()
     first_direction()
     first_image()
+    north_forward()
     first_coarse()
-    east_first()
     first_applied()
     first_sums()
+    east_first()
+    first_spread()
     second_image()
     second_coarse()
     first_step()
+    second_sums()
+    second_spread()
     east_second()
-    second_sums()
     second_step()
     shape_spectrum()
     east_back()
     east_last()
     north_back()
 
-    for buf, phase in ((in1, T1), (send3, T2B), (send4, T3P), (xp, RP), (xq, RQ), (r1, R1), (r2, R2)):
+    for buf, phase in ((in1, T1), (send5, T3Q), (r1, R1), (r2, R2)):
         left(buf.at[pl.ds(0, ROWS - 1)], phase)
-    for buf, phase in ((send2, T2A), (zp, ZP), (zq, ZQ), (z1, Z1), (z2, Z2)):
+    for buf, phase in ((send2, T2A), (send4, T3P), (zp, ZP), (zq, ZQ), (z1, Z1), (z2, Z2)):
         left(buf.at[pl.ds(0, COLS - 1)], phase)
 
-    left(send5.at[pl.ds(0, 7)], T3Q)
-    left(send5.at[0, pl.ds(0, 56)], T3Q)
-
-    @pl.when((c == 0) & (low2 == 0))
+    for buf, phase, later in ((xp, RP, RP2), (xq, RQ, RQ2)):
+        left(buf.at[0, pl.ds(0, ROWS // 2 - 1)], phase)
+        left(buf.at[0], later)
+
+    @pl.when(group == c)
+    def _():
+        left(send3.at[pl.ds(0, ROWS - 1)], T2B)
+
+    @pl.when(group != c)
+    def _():
+        left(send3, T2B)
+
+    @pl.when((c == 0) & (r == 0))
     def _():
         left(twin_send.at[pl.ds(0, 7)], TWIN)
 
-    @pl.when((c == 0) & (low2 != 0))
+    @pl.when((c == 0) & (r != 0))
     def _():
         left(twin_send, TWIN)
 
@@ -864,6 +889,11 @@
     halo_left(p_own, halo0, COLLECT0, True)
     halo_left(spread1.at[4], ret1, RETURN1, False)
     halo_left(q_own, halo1, COLLECT1, True)
+
+
+def settle(coef_in, map_in, coef_out, map_out):
+    coef_out[...] = coef_in[...]
+    map_out[...] = map_in[...]
 
 
 def on_device(
@@ -888,18 +918,18 @@
     scratch += [pltpu.VMEM(shape, kind) for shape, kind in zip(shapes, kinds)]
     scratch += [
         v(*block), v(8, 32, 256), v(8, 32, 256), v(*block), v(*block),
-        v(8, 16, 128), v(*block), v(*block), v(*block), v(8, 64, 128), v(8, 8, 8, 128),
+        v(8, 16, 128), v(*block), v(8, 64, 128), v(8, 64, 128), v(*block), v(*block),
         v(512, 128), v(512, 128), v(8, 512, 128),
     ]
     scratch += [v(9, 8, 128) for _ in range(7)]
     scratch += [
         v(8, 128), v(8, 128), v(8, 8, 128), v(8, 8, 128),
-        v(16, 256), v(16, 256), v(32, 16, 256), v(32, 16, 256),
+        v(16, 256), v(16, 256), v(2, 16, 16, 256), v(2, 16, 16, 256),
         v(256, 128), v(256, 128), v(8, 128), v(8, 128), v(8, 128), v(8, 128),
         v(8, 8, 128), v(32, 8, 128), v(8, 8, 128), v(32, 8, 128),
     ]
     scratch += [
-        pltpu.SemaphoreType.DMA((15,)),
+        pltpu.SemaphoreType.DMA((13,)),
         pltpu.SemaphoreType.DMA((PHASES,)),
         pltpu.SemaphoreType.DMA((PHASES,)),
         pltpu.SemaphoreType.DMA((4, 9)),
@@ -911,7 +941,7 @@
             jax.ShapeDtypeStruct((1, 1, 512), F32),
             jax.ShapeDtypeStruct((16, FULL), F32),
         ),
-        in_specs=[smem] * 8 + [hbm, vmem, vmem] + [hbm] * len(consts),
+        in_specs=[smem] * 7 + [hbm, vmem, vmem] + [hbm] * len(consts),
         out_specs=(vmem, vmem),
         scratch_shapes=scratch,
         compiler_params=pltpu.CompilerParams(
@@ -920,11 +950,19 @@
     )(
         footprints.reshape(9), counts.reshape(1), damping, layer_depth,
         inclinations, declinations,
-        jnp.asarray(table["twist_coarse"]), jnp.asarray(table["back_coarse"]),
+        jnp.asarray(table["twist_coarse"]),
         kernel_tiles.reshape(9, 256, 512), readings.reshape(1, 256),
         resid_grid.reshape(block), *consts,
     )
-    return coef, rtp_map
+    return pl.pallas_call(
+        settle,
+        out_shape=(
+            jax.ShapeDtypeStruct((1, 1, 512), F32),
+            jax.ShapeDtypeStruct((16, FULL), F32),
+        ),
+        in_specs=[vmem, vmem],
+        out_specs=(vmem, vmem),
+    )(coef, rtp_map)
 
 
 def solution(mesh):

time: 85.1 us -> 71 us (0.83)
  Pallas kernels: 80.1 us -> 68.9 us
  local copies, waits for them, and re-layouts: 2.92 us -> 0 us
    pallas_call x1, Pallas kernels: 80.1 us -> 67.3 us  [on_device(): pl.pallas_call(kernel, out_shape=(jax.ShapeDtypeStruct((1, 1, 512), F32),...]
    unnamed x2 -> x0, local copies, waits for them, and re-layouts: 2.92 us -> none
    pallas_call x0 -> x1, Pallas kernels: none -> 1.68 us  [on_device(): pl.pallas_call(settle, out_shape=(jax.ShapeDtypeStruct((1, 1, 512), F32),...]
where the time goes in v3:
time: 71 us; the launch traced here: 70.9 us
  Pallas kernels  68.9 us (97%)
  between operations  1.93 us (3%)
    pallas_call x1, Pallas kernels, on_device(): pl.pallas_call(kernel, out_shape=(jax.ShapeDtypeStruct((1, 1, 512), F32),...  67.3 us
    pallas_call x1, Pallas kernels, on_device(): pl.pallas_call(settle, out_shape=(jax.ShapeDtypeStruct((1, 1, 512), F32),...  1.68 us

profile of v3, /device:TPU:1, one launch (start us, length us, event | category | flops | bytes accessed | tf_op | source)
XLA Modules:
  0.0 70.9 jit_solution(3970741711589567490)
XLA Ops:
  1.9 67.3 %shard_map.221 = (f32[1,1,512]{2,1,0:T(1,128)}, f32[16,4096]{1,0:T(8,128)}) custom-call(s32[9]{0:T(128)} %bitcast.9, s32[1]{0:T(128)} %bitcast.5.counts, f32[1]{0:T(128)S(6)} %copy.25.damping, f32[2]{0:T(128)} %depth.1, f32[2]{0:T(128)} %inclinations.1, f32[2]{0:T(128)} %declinations.1, f32[32,16]{1,0:T(8,128)} %constant.38.clone.twist_coarse, ...), custom_call_target="tpu_custom_call" | custom-call | tf_op jit(solution)/shard_map/pallas_call | solution.py:938
  69.2 1.7 %shard_map.222 = (f32[1,1,512]{2,1,0:T(1,128)}, f32[16,4096]{1,0:T(8,128)}) custom-call(f32[1,1,512]{2,1,0:T(1,128)} %get-tuple-element.4.coef_in, f32[16,4096]{1,0:T(8,128)} %get-tuple-element.5.map_in), custom_call_target="tpu_custom_call" | custom-call | tf_op jit(solution)/shard_map/pallas_call | solution.py:957

commit v4 on v3

--- a/solution.py
+++ b/solution.py
@@ -20,8 +20,8 @@
 OFFSETS = tuple((a, b) for a in (-1, 0, 1) for b in (-1, 0, 1))
 SCALE = 1.0 / 16777216.0
 
-(T1, T2A, T2B, TWIN, T3P, T3Q, ZP, RP, ZQ, RQ, Z1, R1, Z2, R2, RP2, RQ2) = range(16)
-PHASES = 16
+(T1, T2A, T2B, TWIN, T3P, T3Q, ZP, RP, ZQ, RQ, Z1, R1, Z2, R2, RP2, RQ2, T3P1, T3Q1) = range(18)
+PHASES = 18
 RETURN0, COLLECT0, RETURN1, COLLECT1 = range(4)
 
 
@@ -46,7 +46,8 @@
     inv = np.stack([2 * np.cos(ang_a), -2 * np.sin(ang_a)])
     inv[0, 0] = 1.0
     inv[1, 0] = (-1.0) ** a
-    outer_inv = np.kron(inv.reshape(32, 32).T, eye)
+    outer_inv = np.kron(inv.reshape(32, 32).T, eye).reshape(512, 2, 16, 2, 8)
+    outer_inv = outer_inv.transpose(0, 1, 3, 2, 4).reshape(512, 512)
     ang_t = two_pi * np.outer(ka, n) / 4096
     twist = np.stack([np.cos(ang_t), np.sin(ang_t)])[:, :, None, :]
     th = two_pi * np.outer(n, kn) / 128
@@ -77,7 +78,7 @@
     w = np.arange(512)
     th_w = two_pi * (np.outer(w, w) % 512) / 512
     east = np.concatenate([np.cos(th_w), np.sin(th_w)])
-    back = np.arange(512).reshape(4, 8, 16).transpose(1, 0, 2).reshape(512)
+    back = np.arange(512).reshape(4, 8, 2, 8).transpose(2, 1, 0, 3).reshape(512)
     east_inv = np.concatenate([np.cos(th_w)[back], np.sin(th_w)[back]])
     kb = np.arange(8)
     ang_c = two_pi * np.outer(np.arange(32), 16 * kb) / 4096
@@ -224,10 +225,10 @@
     east_inv,
     in1, send2, in2, send3, in3, twin_send, twin_in, send4, in4, send5, in5,
     spec_main, spec_twin, filt,
-    spread0, spread1, ret0, ret1, halo0, halo1, chosen,
+    spread0, spread1, in_order, ret0, ret1, halo0, halo1, chosen,
     p_own, q_own, zp, zq, xp_send, xq_send, xp, xq,
     y_p, y_q, sum1, sum2, sum1b, sum2b, z1, r1, z2, r2,
-    load_sem, send_sem, recv_sem, halo_send, halo_recv,
+    tile_sem, load_sem, send_sem, recv_sem, halo_send, halo_recv,
 ):
     r = lax.axis_index("row")
     c = lax.axis_index("col")
@@ -236,7 +237,6 @@
     special = r == 0
 
     loads = [
-        (tiles_hbm, tiles),
         (outer_fwd_h, outer_fwd),
         (inner_fwd_h, inner_fwd),
         (first_fwd_h, first_fwd),
@@ -253,7 +253,19 @@
     copies = [
         pltpu.make_async_copy(src, dst, load_sem.at[i]) for i, (src, dst) in enumerate(loads)
     ]
-    copies[0].start()
+
+    def tile_copy(k):
+        return pltpu.make_async_copy(tiles_hbm.at[k], tiles.at[k], tile_sem.at[k])
+
+    for k in range(9):
+        tile_copy(k).start()
+
+    core = r % 2
+    chip = r // 2
+    cols_far = [(c + step) % COLS for step in (4, 3, 5, 2, 6, 1, 7)]
+    along_x = [8 * ((r // 8 + step) % 4) for step in (2, 1, 3, 0)]
+    along_y = [2 * ((chip + step) % 4) for step in (2, 1, 3, 0)]
+    rows_far = [x + y + one for x in along_x for y in along_y for one in (1 - core, core)][:-1]
 
     barrier = pltpu.get_barrier_semaphore()
 
@@ -263,13 +275,10 @@
     def exists(a, b):
         return (r + a >= 0) & (r + a < ROWS) & (c + b >= 0) & (c + b < COLS)
 
-    @pl.loop(1, ROWS)
-    def _(i):
-        greet((r + i) % ROWS, c)
-
-    @pl.loop(1, COLS)
-    def _(i):
-        greet(r, (c + i) % COLS)
+    for row in rows_far:
+        greet(row, c)
+    for col in cols_far:
+        greet(r, col)
 
     expected = jnp.int32(ROWS - 1 + COLS - 1)
     for a in (-1, 1):
@@ -281,7 +290,6 @@
             def _():
                 greet(r + a, c + b)
 
-
     def push(src, dst, phase, row, col):
         pltpu.make_async_remote_copy(
             src_ref=src, dst_ref=dst, send_sem=send_sem.at[phase], recv_sem=recv_sem.at[phase],
@@ -297,50 +305,28 @@
     def left(ref, phase):
         pltpu.make_async_copy(ref, ref, send_sem.at[phase]).wait()
 
-    def far_col(j):
-        half = (j + 1) // 2
-        return (c + jnp.where(j % 2 == 1, 4 - half, 4 + half)) % COLS
-
-    def far_row(j):
-        def step(i):
-            return jnp.where(i == 0, 2, jnp.where(i == 3, 0, 2 * i - 1))
-
-        x = (r // 8 + step(j // 8)) % 4
-        y = (r // 2 + step(j // 2 % 4)) % 4
-        return 8 * x + 2 * y + (r + 1 + j) % 2
-
     def rows_exchange(src, dst, phase):
         keep(src.at[r], dst.at[r], phase)
 
-        @pl.loop(0, ROWS - 1)
-        def _(i):
-            row = far_row(i)
+        for row in rows_far:
             push(src.at[row], dst.at[r], phase, row, c)
 
     def cols_exchange(src, dst, phase):
         keep(src.at[c], dst.at[c], phase)
 
-        @pl.loop(0, COLS - 1)
-        def _(i):
-            col = far_col(i)
+        for col in cols_far:
             push(src.at[col], dst.at[c], phase, r, col)
 
     def rows_share(src, dst, phase):
         keep(src, dst.at[r], phase)
-
-        @pl.loop(0, ROWS - 1)
-        def _(i):
-            push(src, dst.at[r], phase, far_row(i), c)
-
-    core = r % 2
-    chip = r // 2
+        for row in rows_far:
+            push(src, dst.at[r], phase, row, c)
 
     def chips_share(src, dst, phase):
         keep(src, dst.at[core, chip], phase)
 
-        @pl.loop(0, ROWS // 2 - 1)
-        def _(i):
-            push(src, dst.at[core, chip], phase, far_row(2 * i + 1), c)
+        for row in rows_far[1::2]:
+            push(src, dst.at[core, chip], phase, row, c)
 
     def chip_share(dst, phase_in, phase_out):
         arrived(dst.at[core], phase_in)
@@ -349,9 +335,8 @@
     def cols_share(src, dst, phase):
         keep(src, dst.at[c], phase)
 
-        @pl.loop(0, COLS - 1)
-        def _(i):
-            push(src, dst.at[c], phase, r, far_col(i))
+        for col in cols_far:
+            push(src, dst.at[c], phase, r, col)
 
     def halo_copy(src, dst, turn, code, row, col):
         return pltpu.make_async_remote_copy(
@@ -401,21 +386,27 @@
 
     sub8 = lax.broadcasted_iota(jnp.int32, (8, 128), 0)
 
+    def place_of(code):
+        k = jnp.int32(0)
+        for j in range(9):
+            k = jnp.where(foot[j] == code, j, k)
+        return k
+
+    def block_of(k, y):
+        total = jnp.zeros((8, 128), F32)
+        for m in range(4):
+            acc = [jnp.zeros((8, 128), F32) for _ in range(4)]
+            for t in range(32):
+                part = tiles[k, pl.ds(8 * t, 8), pl.ds(128 * m, 128)]
+                acc[t % 4] = acc[t % 4] + part * y[pl.ds(8 * t, 8), :]
+            row = jnp.sum((acc[0] + acc[1]) + (acc[2] + acc[3]), axis=0, keepdims=True)
+            total = total + jnp.where(sub8 == m, jnp.broadcast_to(row, (8, 128)), 0.0)
+        return total
+
     def spread_of(y, out):
         @pl.loop(0, 9)
         def _(code):
-            k = jnp.int32(0)
-            for j in range(9):
-                k = jnp.where(foot[j] == code, j, k)
-            total = jnp.zeros((8, 128), F32)
-            for m in range(4):
-                acc = [jnp.zeros((8, 128), F32) for _ in range(4)]
-                for t in range(32):
-                    part = tiles[k, pl.ds(8 * t, 8), pl.ds(128 * m, 128)]
-                    acc[t % 4] = acc[t % 4] + part * y[pl.ds(8 * t, 8), :]
-                row = jnp.sum((acc[0] + acc[1]) + (acc[2] + acc[3]), axis=0, keepdims=True)
-                total = total + jnp.where(sub8 == m, jnp.broadcast_to(row, (8, 128)), 0.0)
-            out[code] = total
+            out[code] = block_of(place_of(code), y)
 
     def readings_of(blocks, y):
         @pl.loop(0, 8)
@@ -452,16 +443,16 @@
 
     lane8 = lanes_of((8, 128))
 
+    lane1 = lanes_of((1, 128))
+
     def pack(parts):
-        out = jnp.zeros((8, 128), F32)
+        out = jnp.zeros((1, 128), F32)
         for i, part in enumerate(parts):
-            out = out + jnp.where(
-                (lane8 == i) & (sub8 == 0), jnp.broadcast_to(part, (8, 128)), 0.0
-            )
+            out = jnp.where(lane1 == i, jnp.broadcast_to(part, (1, 128)), out)
         return out
 
     def unpack(x, i):
-        return total_of(jnp.where((lane8 == i) & (sub8 == 0), x, 0.0))
+        return jnp.sum(jnp.where(lane1 == i, x, 0.0), axis=1, keepdims=True)
 
     state = {}
     sign512 = signs_of((512, 128))
@@ -483,18 +474,25 @@
         y_q[...] = jnp.where(
             slot_index < counts[0], jnp.broadcast_to(column, (SLOTS, 128)), 0.0
         )
-        copies[0].wait()
-        for one in copies[1:]:
+        for one in copies:
             one.start()
-        spread_of(y_q, spread0)
+
+        @pl.loop(0, 9)
+        def _(k):
+            tile_copy(k).wait()
+            in_order[k] = block_of(k, y_q)
+
+        @pl.loop(0, 9)
+        def _(code):
+            spread0[code] = in_order[place_of(code)]
 
     def right_side_return():
         return_start(spread0, ret0, RETURN0)
 
     def north_forward():
-        for i in range(1, 4):
+        for i in range(0, 3):
             copies[i].wait()
-        copies[4].wait()
+        copies[3].wait()
         arrived(in1, T1)
         outer = dot3(
             (outer_fwd[0], outer_fwd[1]), split(in1[...].reshape(512, 128))
@@ -550,7 +548,7 @@
         chips_share(xp_send, xp, RP)
 
     def east_first():
-        copies[5].wait()
+        copies[4].wait()
         arrived(in2, T2A)
         pairs = short_transform(
             [(in2[b, :, 0:128], in2[b, :, 128:256]) for b in range(8)], -1.0
@@ -581,7 +579,8 @@
 
         @pl.loop(0, ROWS)
         def _(i):
-            k = far_col(i // 4)
+            half = (i // 4 + 1) // 2
+            k = (c + jnp.where(i // 4 % 2 == 1, 4 - half, 4 + half)) % COLS
             low = (low2 + i) % 4
             block = send3.at[4 * k + low]
 
@@ -605,12 +604,15 @@
                 def _():
                     push(twin_send.at[k], twin_in.at[r], TWIN, 0, k)
 
+    def sum_of(x, count):
+        total = x[0]
+        for i in range(1, count):
+            total = total + x[i]
+        return total
+
     def share_sums(z, mine, out, phase_in, phase_out):
         arrived(z, phase_in)
-        half_sum = z[0]
-        for i in range(1, 8):
-            half_sum = half_sum + z[i]
-        mine[...] = half_sum
+        mine[...] = sum_of(z, COLS)
         rows_share(mine, out, phase_out)
 
     def first_applied():
@@ -708,7 +710,7 @@
                 filt[4 + i, pl.ds(base, 32), :] = twin
 
     def east_second():
-        copies[6].wait()
+        copies[5].wait()
         arrived(in3, T2B)
 
         @pl.when(special)
@@ -746,9 +748,9 @@
         state.update(alpha=step0 + step1 + step1 * beta, gamma=-step1 * step0)
 
     def shape_spectrum():
+        copies[6].wait()
         copies[7].wait()
-        copies[8].wait()
-        copies[12].wait()
+        copies[11].wait()
         alpha, gamma = state["alpha"], state["gamma"]
         rows_of = []
         extra = []
@@ -784,46 +786,58 @@
     def east_back():
         spun = dot3((east_inv[0], east_inv[1]), split(state["shaped"]))
         back = spun[:512] - sign512 * swap(spun[512:])
-        sign16 = signs_of((16, 128))
-        fine_c, fine_s = twist_fine[0, c], twist_fine[1, c]
-        for mid in range(8):
-            for top in range(4):
-                base = 64 * mid + 16 * top
-                block = back[base:base + 16]
-                co = twist_coarse[8 * top + mid, c]
-                si = twist_coarse[8 * top + mid, 8 + c]
-                tc = co * fine_c - si * fine_s
-                ts = si * fine_c + co * fine_s
-                send4[mid, 16 * top:16 * top + 16, :] = block * tc - sign16 * ts * swap(block)
-        cols_exchange(send4, in4, T3P)
+        sign8 = signs_of((8, 128))
+        for half in range(2):
+            rows = slice(8 * half, 8 * half + 8)
+            fine_c, fine_s = twist_fine[0, c, rows, :], twist_fine[1, c, rows, :]
+            for mid in range(8):
+                for top in range(4):
+                    base = 256 * half + 32 * mid + 8 * top
+                    block = back[base:base + 8]
+                    co = twist_coarse[8 * top + mid, c]
+                    si = twist_coarse[8 * top + mid, 8 + c]
+                    tc = co * fine_c - si * fine_s
+                    ts = si * fine_c + co * fine_s
+                    send4[half, mid, 8 * top:8 * top + 8, :] = (
+                        block * tc - sign8 * ts * swap(block)
+                    )
+            cols_exchange(send4.at[half], in4.at[half], (T3P, T3P1)[half])
 
     def east_last():
-        arrived(in4, T3P)
-        for pair in range(2):
-            values = []
-            for k in range(8):
-                m0 = in4[k, 32 * pair:32 * pair + 16, :]
-                m1 = in4[k, 32 * pair + 16:32 * pair + 32, :]
-                values.append((jnp.where(left16, m0, swap(m1)), jnp.where(left16, swap(m0), m1)))
-            for b, (re, im) in enumerate(short_transform(values, 1.0)):
-                send5[4 * b + 2 * pair] = jnp.where(left16, re, swap(im))
-                send5[4 * b + 2 * pair + 1] = jnp.where(left16, swap(re), im)
-        rows_exchange(send5, in5, T3Q)
+        left8 = lanes_of((8, 128)) < 64
+        for half in range(2):
+            arrived(in4.at[half], (T3P, T3P1)[half])
+            for pair in range(2):
+                values = []
+                for k in range(8):
+                    m0 = in4[half, k, 16 * pair:16 * pair + 8, :]
+                    m1 = in4[half, k, 16 * pair + 8:16 * pair + 16, :]
+                    values.append(
+                        (jnp.where(left8, m0, swap(m1)), jnp.where(left8, swap(m0), m1))
+                    )
+                for b, (re, im) in enumerate(short_transform(values, 1.0)):
+                    send5[half, 4 * b + 2 * pair] = jnp.where(left8, re, swap(im))
+                    send5[half, 4 * b + 2 * pair + 1] = jnp.where(left8, swap(re), im)
+            rows_exchange(send5.at[half], in5.at[half], (T3Q, T3Q1)[half])
 
     def north_back():
-        for i in range(9, 12):
+        for i in range(8, 11):
             copies[i].wait()
-        arrived(in5, T3Q)
+        arrived(in5.at[0], T3Q)
+        arrived(in5.at[1], T3Q1)
         tw_c, tw_s = twist[0], twist[1]
-        come = in5[...].reshape(16, 2, 16, 128)
+        come = in5[...].reshape(2, 16, 2, 8, 128)
         pair = jnp.concatenate(
-            [come[:, 0].reshape(256, 128), come[:, 1].reshape(256, 128)], axis=1
-        )
-        pair_h, pair_l = split(pair)
-        inner = dot3((pair_h, pair_l), (inner_inv[0], inner_inv[1]))
-        first = dot3((pair_h[:16], pair_l[:16]), (first_inv[0], first_inv[1]))
-        inner = jnp.concatenate([first, inner[16:]], axis=0)
-        re, im = inner[:, :128].reshape(16, 16, 128), inner[:, 128:].reshape(16, 16, 128)
+            [come[:, :, 0].reshape(256, 128), come[:, :, 1].reshape(256, 128)], axis=1
+        )
+        inner = dot3(split(pair), (inner_inv[0], inner_inv[1]))
+        lead = jnp.concatenate([pair[0:8], pair[128:136]], axis=0)
+        first = dot3(split(lead), (first_inv[0], first_inv[1]))
+        inner = jnp.concatenate(
+            [first[:8], inner[8:128], first[8:], inner[136:]], axis=0
+        )
+        re = inner[:, :128].reshape(2, 16, 8, 128)
+        im = inner[:, 128:].reshape(2, 16, 8, 128)
         turned = jnp.concatenate(
             [
                 (re * tw_c - im * tw_s).reshape(256, 128),
@@ -859,10 +873,9 @@
     east_back()
     east_last()
     north_back()
-
-    for buf, phase in ((in1, T1), (send5, T3Q), (r1, R1), (r2, R2)):
+    for buf, phase in ((in1, T1), (send5.at[0], T3Q), (send5.at[1], T3Q1), (r1, R1), (r2, R2)):
         left(buf.at[pl.ds(0, ROWS - 1)], phase)
-    for buf, phase in ((send2, T2A), (send4, T3P), (zp, ZP), (zq, ZQ), (z1, Z1), (z2, Z2)):
+    for buf, phase in ((send2, T2A), (send4.at[0], T3P), (send4.at[1], T3P1), (zp, ZP), (zq, ZQ), (z1, Z1), (z2, Z2)):
         left(buf.at[pl.ds(0, COLS - 1)], phase)
 
     for buf, phase, later in ((xp, RP, RP2), (xq, RQ, RQ2)):
@@ -918,18 +931,20 @@
     scratch += [pltpu.VMEM(shape, kind) for shape, kind in zip(shapes, kinds)]
     scratch += [
         v(*block), v(8, 32, 256), v(8, 32, 256), v(*block), v(*block),
-        v(8, 16, 128), v(*block), v(8, 64, 128), v(8, 64, 128), v(*block), v(*block),
+        v(8, 16, 128), v(*block), v(2, 8, 32, 128), v(2, 8, 32, 128),
+        v(2, 32, 8, 128), v(2, 32, 8, 128),
         v(512, 128), v(512, 128), v(8, 512, 128),
     ]
-    scratch += [v(9, 8, 128) for _ in range(7)]
+    scratch += [v(9, 8, 128) for _ in range(8)]
     scratch += [
         v(8, 128), v(8, 128), v(8, 8, 128), v(8, 8, 128),
         v(16, 256), v(16, 256), v(2, 16, 16, 256), v(2, 16, 16, 256),
-        v(256, 128), v(256, 128), v(8, 128), v(8, 128), v(8, 128), v(8, 128),
-        v(8, 8, 128), v(32, 8, 128), v(8, 8, 128), v(32, 8, 128),
+        v(256, 128), v(256, 128), v(1, 128), v(1, 128), v(1, 128), v(1, 128),
+        v(8, 1, 128), v(32, 1, 128), v(8, 1, 128), v(32, 1, 128),
     ]
     scratch += [
-        pltpu.SemaphoreType.DMA((13,)),
+        pltpu.SemaphoreType.DMA((9,)),
+        pltpu.SemaphoreType.DMA((12,)),
         pltpu.SemaphoreType.DMA((PHASES,)),
         pltpu.SemaphoreType.DMA((PHASES,)),
         pltpu.SemaphoreType.DMA((4, 9)),

time: 71 us -> 68.8 us (0.969)
  Pallas kernels: 68.9 us -> 66.7 us
    pallas_call x1, Pallas kernels: 67.3 us -> 65.1 us  [on_device(): pl.pallas_call(kernel, out_shape=(jax.ShapeDtypeStruct((1, 1, 512), F32),...]
where the time goes in v4:
time: 68.8 us; the launch traced here: 68.7 us
  Pallas kernels  66.7 us (97%)
  between operations  1.93 us (3%)
    pallas_call x1, Pallas kernels, on_device(): pl.pallas_call(kernel, out_shape=(jax.ShapeDtypeStruct((1, 1, 512), F32),...  65.1 us
    pallas_call x1, Pallas kernels, on_device(): pl.pallas_call(settle, out_shape=(jax.ShapeDtypeStruct((1, 1, 512), F32),...  1.68 us

profile of v4, /device:TPU:1, one launch (start us, length us, event | category | flops | bytes accessed | tf_op | source)
XLA Modules:
  0.0 68.7 jit_solution(14307925221360191958)
XLA Ops:
  1.9 65.1 %shard_map.221 = (f32[1,1,512]{2,1,0:T(1,128)}, f32[16,4096]{1,0:T(8,128)}) custom-call(s32[9]{0:T(128)} %bitcast.9, s32[1]{0:T(128)} %bitcast.5.counts, f32[1]{0:T(128)S(6)} %copy.25.damping, f32[2]{0:T(128)} %depth.1, f32[2]{0:T(128)} %inclinations.1, f32[2]{0:T(128)} %declinations.1, f32[32,16]{1,0:T(8,128)} %constant.38.clone.twist_coarse, ...), custom_call_target="tpu_custom_call" | custom-call | tf_op jit(solution)/shard_map/pallas_call | solution.py:953
  67.0 1.7 %shard_map.222 = (f32[1,1,512]{2,1,0:T(1,128)}, f32[16,4096]{1,0:T(8,128)}) custom-call(f32[1,1,512]{2,1,0:T(1,128)} %get-tuple-element.4.coef_in, f32[16,4096]{1,0:T(8,128)} %get-tuple-element.5.map_in), custom_call_target="tpu_custom_call" | custom-call | tf_op jit(solution)/shard_map/pallas_call | solution.py:972
